TPU v7x, 32 devices: a whole 2x2x4 slice. The times are simulated.
32 devices in a mesh: gx: 4 (over z), gy: 2 (over y), gz: 4 (over x, core).
Axes of the slice: x: 2, y: 2, z: 4, core: 2. Of those that a mesh axis runs over, the one named last changes fastest.
Arguments:
- features: bfloat16 [32, 16, 8, 512], P(None, 'gx', 'gy', 'gz'), may hold values from -6 to 6
- cotangent: bfloat16 [32, 16, 8, 512], P(None, 'gx', 'gy', 'gz'), may hold values from -6 to 6
- w_fine_in: bfloat16 [27, 32, 32], replicated, may hold values from -0.21875 to 0.21875
- w_coarse_in: bfloat16 [27, 32, 128], replicated, may hold values from -0.21875 to 0.21875
- w_coarse_mid: bfloat16 [27, 128, 128], replicated, may hold values from -0.109375 to 0.109375
- w_lift: bfloat16 [128, 32], replicated, may hold values from -0.5 to 0.5
- w_fine_out: bfloat16 [27, 32, 32], replicated, may hold values from -0.21875 to 0.21875
Outputs:
- output: bfloat16 [32, 16, 8, 512], P(None, 'gx', 'gy', 'gz')
- grad_input: bfloat16 [32, 16, 8, 512], P(None, 'gx', 'gy', 'gz')
- grad_fine_in: float32 [27, 32, 32], P(None, 'gx', ('gy', 'gz'))
- grad_coarse_in: float32 [27, 32, 128], P(None, 'gx', ('gy', 'gz'))
- grad_coarse_mid: float32 [27, 128, 128], P(None, 'gx', ('gy', 'gz'))
- grad_lift: float32 [128, 32], P('gx', ('gy', 'gz'))
- grad_fine_out: float32 [27, 32, 32], P(None, 'gx', ('gy', 'gz'))
All inputs are finite; a program needn't handle non-finite values.
Results may differ from a plain program's by a relative error of at most 0.02.
Values may be sent and summed in bfloat16 or wider, within the bound.
A program may use at most 128 MiB of HBM per device.

v0:
```python
import math

import jax
import jax.numpy as jnp
from jax import lax
from jax.experimental import pallas as pl
from jax.experimental.pallas import tpu as pltpu
from jax.sharding import PartitionSpec as P

AXES = ("gx", "gy", "gz")
MESH = pl.DeviceIdType.MESH
DIRECT = 64


def place(flat, counts):
    nx, ny, nz = counts
    return (flat // (ny * nz), (flat // nz) % ny, flat % nz)


def meet(counts, total, me):
    barrier = pltpu.get_barrier_semaphore()

    def greet(k, carry):
        pl.semaphore_signal(
            barrier, inc=1, device_id=place((me + k) % total, counts), device_id_type=MESH
        )
        return carry

    lax.fori_loop(1, total, greet, 0)
    pl.semaphore_wait(barrier, total - 1)


def spread_kernel(counts, each, x_ref, o_ref, local_sem, send_sem, recv_sem, during):
    total = counts[0] * counts[1] * counts[2]
    me = (lax.axis_index("gx") * counts[1] + lax.axis_index("gy")) * counts[2] + lax.axis_index(
        "gz"
    )
    meet(counts, total, me)

    def copy(k):
        peer = (me + k) % total
        return pltpu.make_async_remote_copy(
            src_ref=x_ref.at[peer] if each else x_ref,
            dst_ref=o_ref.at[me],
            send_sem=send_sem.at[k],
            recv_sem=recv_sem.at[k],
            device_id=place(peer, counts),
            device_id_type=MESH,
        )

    def begin(k, carry):
        copy(k).start()
        return carry

    def finish(k, carry):
        copy(k).wait()
        return carry

    lax.fori_loop(1, total, begin, 0)
    own = pltpu.make_async_copy(x_ref.at[me] if each else x_ref, o_ref.at[me], local_sem)
    own.start()
    during()
    own.wait()
    lax.fori_loop(1, total, finish, 0)


def gather_kernel(counts, x_ref, w_mid, w_in, o_ref, mid_back, in_back, *sems):
    wide, narrow = w_mid.shape[2], in_back.shape[2]

    def turn():
        def body(ab, carry):
            for c in range(3):
                rows = slice(c * wide, c * wide + wide)
                mid_back[ab, rows, :] = w_mid[8 - ab, (2 - c) * wide : (3 - c) * wide, :].T
                in_back[ab, rows, :] = w_in[8 - ab, (2 - c) * narrow : (3 - c) * narrow, :].T
            return carry

        lax.fori_loop(0, 9, body, 0)

    spread_kernel(counts, False, x_ref, o_ref, *sems, turn)


def sum_kernel(counts, scale, x_ref, o_ref, landed, *sems):
    spread_kernel(counts, True, x_ref, landed, *sems, lambda: None)
    o_ref[...] = landed[...].astype(jnp.float32).sum(0) * scale


def spread_call(kernel, counts, ident, outs, scratch, name, *args):
    total = counts[0] * counts[1] * counts[2]
    return pl.pallas_call(
        kernel,
        out_shape=outs,
        in_specs=vmem(len(args)),
        out_specs=vmem(len(outs)),
        scratch_shapes=scratch
        + [
            pltpu.SemaphoreType.DMA,
            pltpu.SemaphoreType.DMA((total,)),
            pltpu.SemaphoreType.DMA((total,)),
        ],
        compiler_params=pltpu.CompilerParams(collective_id=ident, has_side_effects=True),
        name=name,
    )(*args)


def extended(cells, sides, width):
    for axis, dim in sides:
        count = lax.axis_size(axis)
        ends = count - 1
        head = lax.slice_in_dim(cells, 0, width, axis=dim)
        tail = lax.slice_in_dim(cells, cells.shape[dim] - width, cells.shape[dim], axis=dim)
        cells = jnp.concatenate(
            [
                lax.ppermute(tail, axis, [(i, (i + 1) % count) for i in range(ends)]),
                cells,
                lax.ppermute(head, axis, [((i + 1) % count, i) for i in range(ends)]),
            ],
            axis=dim,
        )
    return cells


def silu_slope(values):
    sigma = jax.nn.sigmoid(values)
    return sigma * (1.0 + values * (1.0 - sigma))


def conv_valid(padded, weight, form="NCDHW"):
    kernel = weight.reshape(3, 3, 3, weight.shape[1], weight.shape[2])
    result = lax.conv_general_dilated(
        padded[None],
        kernel,
        (1, 1, 1),
        "VALID",
        dimension_numbers=(form, "DHWIO", form),
        preferred_element_type=jnp.float32,
    )
    return result[0]


def flipped(weight):
    return jnp.flip(weight, 0).transpose(0, 2, 1)


def pool_blocks(field):
    chans, depth, height, length = field.shape
    grouped = field.astype(jnp.float32).reshape(
        chans, depth // 4, 4, height // 4, 4, length // 4, 4
    )
    return grouped.sum(axis=(2, 4, 6))


def spread_up(field):
    chans, depth, height, length = field.shape
    grown = jnp.broadcast_to(
        field[:, :, None, :, None, :, None], (chans, depth, 4, height, 4, length, 4)
    )
    return grown.reshape(chans, depth * 4, height * 4, length * 4)


def tap_grad_direct(padded, grad):
    depth = padded.shape[1] - 2
    height = padded.shape[2] - 2
    length = padded.shape[3] - 2
    flat_grad = grad.reshape(grad.shape[0], -1)
    blocks = []
    for tap in range(27):
        shift_x, shift_y, shift_z = (tap // 9, tap // 3 % 3, tap % 3)
        window = padded[
            :, shift_x : shift_x + depth, shift_y : shift_y + height, shift_z : shift_z + length
        ].reshape(padded.shape[0], -1)
        blocks.append(
            lax.dot_general(
                window, flat_grad, (((1,), (1,)), ((), ())), preferred_element_type=jnp.float32
            )
        )
    return jnp.stack(blocks)


def fine_rim(field):
    return extended(field, (("gx", 1), ("gy", 2), ("gz", 3)), 1)


def coarse_rim(field):
    return extended(field, (("gx", 1), ("gy", 2), ("gz", 3)), 1)


def reduce_grad(partial_value):
    first = lax.psum_scatter(partial_value, "gx", scatter_dimension=1, tiled=True)
    return lax.psum_scatter(first, ("gy", "gz"), scatter_dimension=2, tiled=True)


def input_share(field):
    parts = lax.all_to_all(field[None], "gx", split_axis=1, concat_axis=0, tiled=True)
    moved = jnp.moveaxis(parts, 0, 1)
    moved = moved.reshape(moved.shape[0], -1, moved.shape[3], moved.shape[4])
    moved = lax.all_gather(moved, "gy", axis=2, tiled=True)
    return lax.all_gather(moved, "gz", axis=3, tiled=True)


def output_share(field):
    parts = lax.all_to_all(field[None], ("gy", "gz"), split_axis=1, concat_axis=0, tiled=True)
    count_y = lax.axis_size("gy")
    count_z = lax.axis_size("gz")
    chans = parts.shape[1]
    depth, height, length = (parts.shape[2], parts.shape[3], parts.shape[4])
    grid = parts.reshape(count_y, count_z, chans, depth, height, length).transpose(2, 3, 0, 4, 1, 5)
    grid = grid.reshape(chans, depth, count_y * height, count_z * length)
    return lax.all_gather(grid, "gx", axis=1, tiled=True)


def shards_layered(features, cotangent, w_fine_in, w_coarse_in, w_coarse_mid, w_lift, w_fine_out):
    depth, height, length = (features.shape[1], features.shape[2], features.shape[3])
    whole_cells = (
        depth * lax.axis_size("gx") * height * lax.axis_size("gy") * length * lax.axis_size("gz")
    )
    scale = 1.0 / math.sqrt(whole_cells)
    padded_in = fine_rim(features)
    z_first = conv_valid(padded_in, w_fine_in)
    act_first = jax.nn.silu(z_first).astype(jnp.bfloat16)
    pooled = (pool_blocks(act_first) / 64.0).astype(jnp.bfloat16)
    pooled_pad = coarse_rim(pooled)
    z_second = conv_valid(pooled_pad, w_coarse_in)
    act_second = jax.nn.silu(z_second).astype(jnp.bfloat16)
    second_pad = coarse_rim(act_second)
    z_third = conv_valid(second_pad, w_coarse_mid)
    act_third = jax.nn.silu(z_third).astype(jnp.bfloat16)
    lifted = lax.dot_general(
        w_lift, act_third, (((0,), (0,)), ((), ())), preferred_element_type=jnp.float32
    )
    joined = (act_first.astype(jnp.float32) + spread_up(lifted)).astype(jnp.bfloat16)
    padded_joined = fine_rim(joined)
    output = conv_valid(padded_joined, w_fine_out).astype(jnp.bfloat16)
    part_fine_out = tap_grad_direct(padded_joined, cotangent) * scale
    d_joined = conv_valid(fine_rim(cotangent), flipped(w_fine_out))
    d_lift = pool_blocks(d_joined)
    lift_partial = (
        lax.dot_general(
            act_third.astype(jnp.float32),
            d_lift,
            (((1, 2, 3), (1, 2, 3)), ((), ())),
            precision=lax.Precision.HIGHEST,
        )
        * scale
    )
    d_third = lax.dot_general(
        w_lift.astype(jnp.float32),
        d_lift,
        (((1,), (0,)), ((), ())),
        precision=lax.Precision.HIGHEST,
    )
    dz_third = (d_third * silu_slope(z_third)).astype(jnp.bfloat16)
    dz_third_pad = coarse_rim(dz_third)
    grad_coarse_mid = None
    sources = input_share(act_second)
    sources_pad = jnp.pad(sources, ((0, 0), (1, 1), (1, 1), (1, 1)))
    targets = output_share(dz_third)
    grad_coarse_mid = tap_grad_direct(sources_pad, targets) * scale
    dz_second = (conv_valid(dz_third_pad, flipped(w_coarse_mid)) * silu_slope(z_second)).astype(
        jnp.bfloat16
    )
    dz_second_pad = coarse_rim(dz_second)
    part_coarse_in = tap_grad_direct(pooled_pad, dz_second) * scale
    d_pool = conv_valid(dz_second_pad, flipped(w_coarse_in))
    dz_first = ((d_joined + spread_up(d_pool) / 64.0) * silu_slope(z_first)).astype(jnp.bfloat16)
    part_fine_in = tap_grad_direct(padded_in, dz_first) * scale
    grad_input = conv_valid(fine_rim(dz_first), flipped(w_fine_in)).astype(jnp.bfloat16)
    pending = [part_fine_out, lift_partial[None], part_coarse_in, part_fine_in]
    reduced = [reduce_grad(partial_value) for partial_value in pending]
    grad_fine_out = reduced[0]
    grad_lift = reduced[1][0]
    grad_coarse_in = reduced[2]
    grad_fine_in = reduced[3]
    return (
        output,
        grad_input,
        grad_fine_in,
        grad_coarse_in,
        grad_coarse_mid,
        grad_lift,
        grad_fine_out,
    )


def halo_kernel(counts, x_ref, o_ref, rows, packed, from_low, from_high, sends, recvs):
    nx, ny, nz = counts
    gx, gy, gz = (lax.axis_index(axis) for axis in AXES)
    sides = [(i, j, 0) for i in (-1, 0, 1) for j in (-1, 0, 1) if (i, j) != (0, 0)]
    sides += [(0, 0, -1), (0, 0, 1)]

    def there(side, sign):
        x, y, z = gx + sign * side[0], gy + sign * side[1], gz + sign * side[2]
        real = (x >= 0) & (x < nx) & (y >= 0) & (y < ny) & (z >= 0) & (z < nz)
        return (x, y, z), real

    rows[...] = jnp.zeros_like(rows)
    from_low[...] = jnp.zeros_like(from_low)
    from_high[...] = jnp.zeros_like(from_high)
    barrier = pltpu.get_barrier_semaphore()
    met = 0
    for side in sides:
        peer, real = there(side, 1)
        met = met + jnp.where(real, 1, 0)

        @pl.when(real)
        def _():
            pl.semaphore_signal(barrier, inc=1, device_id=peer, device_id_type=MESH)

    pl.semaphore_wait(barrier, met)
    d, h = x_ref.shape[:2]
    take = {-1: lambda n: pl.ds(0, 2), 0: lambda n: pl.ds(0, n), 1: lambda n: pl.ds(n - 2, 2)}
    land = {-1: lambda n: pl.ds(n + 2, 2), 0: lambda n: pl.ds(2, n), 1: lambda n: pl.ds(0, 2)}

    def transfer(k, side):
        if k < 8:
            source = x_ref.at[take[side[0]](d), take[side[1]](h)]
            target = rows.at[land[side[0]](d), land[side[1]](h)]
        else:
            source, target = packed, (from_high if side[2] < 0 else from_low)
        return pltpu.make_async_remote_copy(
            src_ref=source,
            dst_ref=target,
            send_sem=sends.at[k],
            recv_sem=recvs.at[k],
            device_id=there(side, 1)[0],
            device_id_type=MESH,
        )

    def run(first, last):
        for k in range(first, last):

            @pl.when(there(sides[k], 1)[1])
            def _():
                transfer(k, sides[k]).start()

    def settle(first, last):
        for k in range(first, last):

            @pl.when(there(sides[k], -1)[1])
            def _():
                transfer(k, sides[k]).wait_recv()

            @pl.when(there(sides[k], 1)[1])
            def _():
                transfer(k, sides[k]).wait_send()

    run(0, 8)
    settle(0, 8)
    rows[2 : 2 + d, 2 : 2 + h] = x_ref[...]
    lane = lax.broadcasted_iota(jnp.int32, (x_ref.shape[2], 128), 1)
    spots = [(x, y) for x in range(d + 4) for y in range(h + 4)]
    for part in range(2):
        group = jnp.zeros(lane.shape, jnp.float32)
        for r in range(32):
            x, y = spots[part * 32 + r]
            turned = pltpu.roll(rows[x, y].astype(jnp.float32), (2 + 4 * r) % 128, 1)
            group = jnp.where(lane // 4 == r, turned, group)
        packed[:, part * 128 : part * 128 + 128] = group.astype(jnp.bfloat16)
    run(8, 10)
    for x, y in spots:
        o_ref[x, y, :, 0:128] = rows[x, y]
    settle(8, 10)
    for part in range(2):
        span = slice(part * 128, part * 128 + 128)
        group = jnp.where(
            lane % 4 >= 2,
            from_high[:, span].astype(jnp.float32),
            from_low[:, span].astype(jnp.float32),
        )
        for r in range(32):
            x, y = spots[part * 32 + r]
            o_ref[x, y, :, 128:256] = pltpu.roll(group, 126 - 4 * r if r < 32 else 0, 1).astype(
                jnp.bfloat16
            )


def vmem(count):
    return [pl.BlockSpec(memory_space=pltpu.VMEM)] * count


ROOMY = 60 * 1024 * 1024


def halo(x, counts, ident):
    d, h, chans, length = x.shape
    edge = pltpu.VMEM((chans, 256), jnp.bfloat16)
    return pl.pallas_call(
        lambda *refs: halo_kernel(counts, *refs),
        out_shape=jax.ShapeDtypeStruct((d + 4, h + 4, chans, 256), x.dtype),
        in_specs=vmem(1),
        out_specs=vmem(1)[0],
        scratch_shapes=[
            pltpu.VMEM((d + 4, h + 4, chans, length), x.dtype),
            edge,
            edge,
            edge,
            pltpu.SemaphoreType.DMA((10,)),
            pltpu.SemaphoreType.DMA((10,)),
        ],
        compiler_params=pltpu.CompilerParams(
            collective_id=ident, has_side_effects=True, vmem_limit_bytes=ROOMY
        ),
        name="halo",
    )(x)


def stacked(value):
    size = value.shape[1]
    return jnp.concatenate(
        [pltpu.roll(value, 1, 1), value, pltpu.roll(value, size - 1, 1)]
    ).astype(jnp.bfloat16)


def around(ref, x, y, rows, lanes):
    return jnp.concatenate(
        [ref[x + a, y + b, rows, lanes] for a in range(3) for b in range(3)]
    )


def dot(a, b):
    return jnp.dot(a, b, preferred_element_type=jnp.float32)


def dot_over(a, b, dims, precision=None):
    return lax.dot_general(
        a, b, ((dims[:1], dims[1:]), ((), ())), precision=precision, preferred_element_type=jnp.float32
    )


def ahead(weight):
    return weight[...].reshape(27 * weight.shape[1], weight.shape[2]).T


def back(weight):
    return jnp.concatenate([weight[26 - t] for t in range(27)], axis=1)


def grouped(count, size, body):
    def several(g, carry):
        for i in range(size):
            body(g * size + i, carry)
        return carry

    lax.fori_loop(0, count // size, several, 0)


def fine_kernel(ext, w_in, w_out, z_ref, d_ref, mine, taps, total, ws):
    ws[0], ws[1] = ahead(w_in), back(w_out)

    def fill(r, carry):
        x, y = r // 8, r % 8
        for f in range(2):
            value = ext[x, y, f * 32 : f * 32 + 32, :].astype(jnp.float32)
            taps[x, y, f * 96 : f * 96 + 96, :] = stacked(value)
        return carry

    grouped(64, 4, fill)
    total[...] = jnp.zeros_like(total)

    def body(r, carry):
        x, y = r // 6, r % 6
        z = dot(ws[0], around(taps, x, y, slice(0, 96), slice(None)))
        d = dot(ws[1], around(taps, x, y, slice(96, 192), slice(None)))
        z_ref[x, y] = z
        d_ref[x, y] = d
        act = jax.nn.silu(z[:, :128]).astype(jnp.bfloat16).astype(jnp.float32)
        own = jnp.where((x >= 1) & (x <= 4) & (y >= 1) & (y <= 4), 1.0, 0.0)
        total[...] += own * jnp.concatenate([act, d[:, :128]])
        return carry

    grouped(36, 6, body)
    row = lax.broadcasted_iota(jnp.int32, (32, 128), 0)
    lane = lax.broadcasted_iota(jnp.int32, (32, 128), 1)
    pick = jnp.where(lane // 4 == row, 1.0, 0.0)
    sums = dot_over(pick, total[...], (1, 1), lax.Precision.HIGHEST)
    both = jnp.concatenate([sums[:, :32] * (1.0 / 64.0), sums[:, 32:]], axis=1)
    mine[...] = jnp.concatenate([both[:16], both[16:]], axis=1).astype(jnp.bfloat16)


def coarse_kernel(
    counts, scale, full, w_in, w_mid, w_lift, w_mid_back, w_in_back,
    grown, g_mid, g_in, g_lift,
    pad_in, pad_mid, pad_smid, pad_sin, table,
):
    nx, ny, nz = counts
    cells = nx * ny * 128
    gx, gy, gz = (lax.axis_index(axis) for axis in AXES)
    for pad in (pad_in, pad_mid, pad_smid, pad_sin):
        pad[...] = jnp.zeros_like(pad)

    def pick(size, parts, index):
        each = size // parts
        row = lax.broadcasted_iota(jnp.int32, (size, each), 0)
        column = lax.broadcasted_iota(jnp.int32, (size, each), 1)
        return jnp.where(row == index * each + column, 1.0, 0.0).astype(jnp.bfloat16)

    at_o = gy * nz + gz
    pick_mid, pick_in = pick(128, nx, gx), pick(32, nx, gx)
    pick_o, pick_lift = pick(128, ny * nz, at_o), pick(32, ny * nz, at_o)

    def fill(pad, value):
        at = lax.broadcasted_iota(jnp.int32, value.shape, 0) % 128
        low = jnp.where(at == 0, 0.0, pltpu.roll(value, 1, 0))
        high = jnp.where(at == 127, 0.0, pltpu.roll(value, cells - 1, 0))
        wide = jnp.concatenate([low, value, high], axis=1).astype(jnp.bfloat16)
        pad[1 : nx + 1, 1 : ny + 1] = wide.reshape(nx, ny, 128, wide.shape[1])

    def window(pad, ab):
        a, b = ab // 3, ab % 3
        return pad[a : a + nx, b : b + ny].reshape(cells, pad.shape[3])

    def conv(pad, weight):
        result = dot(window(pad, 0), weight[0])
        for ab in range(1, 9):
            result = result + dot(window(pad, ab), weight[ab])
        return result

    def slope(v):
        sigma = jax.nn.sigmoid(v)
        return sigma * (1.0 + v * (1.0 - sigma))

    pieces = []
    for k in range(nx * ny):
        for z in range(nz):
            block = full[k * nz + z]
            pieces += [block[:, :64], block[:, 64:]]
    both = jnp.concatenate(pieces)
    pooled, d_lift = both[:, :32], both[:, 32:]
    fill(pad_in, pooled.astype(jnp.float32))
    z_second = conv(pad_in, w_in)
    act_second = jax.nn.silu(z_second)
    fill(pad_mid, act_second)
    z_third = conv(pad_mid, w_mid)
    act_third = jax.nn.silu(z_third).astype(jnp.bfloat16)
    lifted = dot(act_third, w_lift[...])
    dz_third = (dot_over(d_lift, w_lift[...], (1, 1)) * slope(z_third)).astype(jnp.bfloat16)
    fill(pad_mid, dz_third.astype(jnp.float32))
    dz_second = (conv(pad_mid, w_mid_back) * slope(z_second)).astype(jnp.bfloat16)
    fill(pad_mid, dz_second.astype(jnp.float32))
    d_pool = conv(pad_mid, w_in_back)

    table[...] = (
        jnp.concatenate([lifted, d_pool * (1.0 / 64.0)], axis=1)
        .astype(jnp.bfloat16)
        .reshape(nx, ny, 128, 64)
    )
    row = lax.broadcasted_iota(jnp.int32, (128, 256), 0)
    lane = lax.broadcasted_iota(jnp.int32, (128, 256), 1)
    cell = jnp.where(lane < 192, lane // 4, -1) + gz * 32
    grow = jnp.where(row == cell, 1.0, 0.0).astype(jnp.bfloat16)
    for i in range(3):
        for j in range(3):
            x = jnp.clip(gx + i - 1, 0, nx - 1)
            y = jnp.clip(gy + j - 1, 0, ny - 1)
            grown[i, j] = dot_over(table[x, y], grow, (0, 0))

    third_o = dot(dz_third, pick_o).T.astype(jnp.bfloat16)
    second_o = dot(dz_second, pick_o).T.astype(jnp.bfloat16)
    fill(pad_smid, dot(act_second.astype(jnp.bfloat16), pick_mid))
    fill(pad_sin, dot(pooled, pick_in))
    for ab in range(9):
        g_mid[ab] = dot(third_o, window(pad_smid, ab)) * scale
        g_in[ab] = dot(second_o, window(pad_sin, ab)) * scale
    third_i = dot(act_third, pick_mid).astype(jnp.bfloat16)
    lift_o = dot(d_lift, pick_lift).T.astype(jnp.bfloat16)
    g_lift[...] = dot(lift_o, third_i) * scale


def last_kernel(
    counts, ext, z_ref, d_ref, grown, w_out, w_in, out, g_input, parts, tj, td, tf, sums, ws
):
    ws[0], ws[1] = ahead(w_out), back(w_in)
    nx, ny, nz = counts
    gx, gy, gz = (lax.axis_index(axis) for axis in AXES)
    lane = lax.broadcasted_iota(jnp.int32, (32, 256), 1)
    at_z = gz * 128 + jnp.where(lane < 192, lane, lane - 256)
    keep_z = jnp.where((at_z >= 0) & (at_z < nz * 128), 1.0, 0.0)

    def fill(r, carry):
        x, y = r // 6, r % 6
        at_x, at_y = gx * 4 + x - 1, gy * 4 + y - 1
        real = (at_x >= 0) & (at_x < nx * 4) & (at_y >= 0) & (at_y < ny * 4)
        keep = keep_z * jnp.where(real, 1.0, 0.0)
        up = grown[(x + 3) // 4, (y + 3) // 4]
        z = z_ref[x, y]
        sigma = jax.nn.sigmoid(z)
        act = (z * sigma).astype(jnp.bfloat16).astype(jnp.float32)
        joined = (act + up[:32]).astype(jnp.bfloat16).astype(jnp.float32) * keep
        dz = (d_ref[x, y] + up[32:]) * (sigma * (1.0 + z * (1.0 - sigma))) * keep
        dz = dz.astype(jnp.bfloat16).astype(jnp.float32)
        tj[x, y] = stacked(joined)[:, :128]
        td[x, y] = stacked(dz)[:, :128]
        tf[x, y] = stacked(ext[x + 1, y + 1, 0:32, :].astype(jnp.float32))[:, :128]
        return carry

    grouped(36, 3, fill)
    sums[...] = jnp.zeros_like(sums)

    def body(r, carry):
        x, y = r // 2, (r % 2) * 2
        whole = slice(None)

        def pair(ref):
            return jnp.concatenate(
                [around(ref, x, y, whole, whole), around(ref, x, y + 1, whole, whole)], axis=1
            )

        near = pair(tj)
        result = dot(ws[0], near).astype(jnp.bfloat16)
        out[x, y], out[x, y + 1] = result[:, :128], result[:, 128:]
        cot = jnp.concatenate(
            [ext[x + 2, y + 2, 32:64, 0:128], ext[x + 2, y + 3, 32:64, 0:128]], axis=1
        )
        sums[0] += dot_over(near, cot, (1, 1))
        result = dot(ws[1], pair(td)).astype(jnp.bfloat16)
        g_input[x, y], g_input[x, y + 1] = result[:, :128], result[:, 128:]
        grad = jnp.concatenate(
            [td[x + 1, y + 1, 32:64, :], td[x + 1, y + 2, 32:64, :]], axis=1
        )
        sums[1] += dot_over(pair(tf), grad, (1, 1))
        return carry

    grouped(8, 2, body)
    ci, co = 32 // nx, 32 // (ny * nz)
    for f in range(2):
        value = sums[f].reshape(27, nx, ci, 32)
        for i in range(nx):
            block = value[:, i].reshape(27 * ci, 32).T
            for j in range(ny * nz):
                parts[i * ny * nz + j, f * co : f * co + co, 0 : 27 * ci] = block[
                    j * co : j * co + co
                ].astype(jnp.bfloat16)


def shards(features, cotangent, w_fine_in, w_coarse_in, w_coarse_mid, w_lift, w_fine_out):
    counts = tuple(lax.axis_size(axis) for axis in AXES)
    nx, ny, nz = counts
    total = nx * ny * nz
    chans, depth, height, length = features.shape
    wide = w_lift.shape[0]
    scale = 1.0 / math.sqrt(total * depth * height * length)
    f32, bf16 = jnp.float32, jnp.bfloat16
    shape = jax.ShapeDtypeStruct
    params = pltpu.CompilerParams(vmem_limit_bytes=ROOMY)

    rows = jnp.concatenate([features, cotangent]).transpose(1, 2, 0, 3)
    ext = halo(rows, counts, 2)
    field = shape((6, 6, chans, 256), f32)
    z_first, d_joined, mine = pl.pallas_call(
        fine_kernel,
        out_shape=(field, field, shape((16, 128), bf16)),
        in_specs=vmem(3),
        out_specs=vmem(3),
        scratch_shapes=[
            pltpu.VMEM((8, 8, 192, 256), bf16),
            pltpu.VMEM((64, 128), f32),
            pltpu.VMEM((2, chans, 27 * chans), bf16),
        ],
        compiler_params=params,
        name="fine",
    )(ext, w_fine_in, w_fine_out)

    w_in9 = w_coarse_in.reshape(9, 3 * chans, wide)
    w_mid9 = w_coarse_mid.reshape(9, 3 * wide, wide)
    full, mid_back, in_back = spread_call(
        lambda *refs: gather_kernel(counts, *refs),
        counts,
        0,
        (
            shape((total,) + mine.shape, bf16),
            shape(w_mid9.shape, bf16),
            shape((9, 3 * wide, chans), bf16),
        ),
        [],
        "gather",
        mine,
        w_mid9,
        w_in9,
    )

    co, cw = wide // (ny * nz), wide // nx
    ci = chans // nx
    pads = [3 * chans, 3 * wide, 3 * cw, 3 * ci]
    grown, g_mid, g_in, g_lift = pl.pallas_call(
        lambda *refs: coarse_kernel(counts, scale, *refs),
        out_shape=(
            shape((3, 3, 2 * chans, 256), f32),
            shape((9, co, 3 * cw), f32),
            shape((9, co, 3 * ci), f32),
            shape((chans // (ny * nz), cw), f32),
        ),
        in_specs=vmem(6),
        out_specs=vmem(4),
        scratch_shapes=[pltpu.VMEM((nx + 2, ny + 2, 128, k), bf16) for k in pads]
        + [pltpu.VMEM((nx, ny, 128, 2 * chans), bf16)],
        compiler_params=params,
        name="coarse",
    )(
        full, w_in9, w_mid9, w_lift, mid_back, in_back
    )

    near = pltpu.VMEM((6, 6, 3 * chans, 128), bf16)
    block = (2 * chans // (ny * nz), 27 * ci)
    output, grad_input, parts = pl.pallas_call(
        lambda *refs: last_kernel(counts, *refs),
        out_shape=(
            shape((4, 4, chans, 128), bf16),
            shape((4, 4, chans, 128), bf16),
            shape((total,) + block, bf16),
        ),
        in_specs=vmem(6),
        out_specs=vmem(3),
        scratch_shapes=[
            near,
            near,
            near,
            pltpu.VMEM((2, 27 * chans, chans), f32),
            pltpu.VMEM((2, chans, 27 * chans), bf16),
        ],
        compiler_params=params,
        name="last",
    )(ext, z_first, d_joined, grown, w_fine_out, w_fine_in)

    (sums,) = spread_call(
        lambda *refs: sum_kernel(counts, scale, *refs),
        counts,
        1,
        (shape(block, f32),),
        [pltpu.VMEM((total,) + block, bf16)],
        "sum_parts",
        parts,
    )
    sums = sums.reshape(2, -1, 27, ci).transpose(0, 2, 3, 1)

    def owned(grad):
        return grad.reshape(9, grad.shape[1], 3, -1).transpose(0, 2, 3, 1).reshape(
            27, -1, grad.shape[1]
        )

    return (
        output.transpose(2, 0, 1, 3),
        grad_input.transpose(2, 0, 1, 3),
        sums[1],
        owned(g_in),
        owned(g_mid),
        g_lift.T,
        sums[0],
    )


def choose(features, *rest):
    nx, ny, nz = (lax.axis_size(axis) for axis in AXES)
    total = nx * ny * nz
    wide = rest[4].shape[0]
    fits = features.shape == (32, 4, 4, 128) and nz == 4 and total <= DIRECT
    fits = fits and 32 % (ny * nz) == 0 and 32 % nx == 0 and 32 // nx == 8 and wide == 128
    return (shards if fits else shards_layered)(features, *rest)


def solution(mesh):
    whole = P(None, "gx", "gy", "gz")
    split = P(None, "gx", ("gy", "gz"))
    return jax.shard_map(
        choose,
        mesh=mesh,
        in_specs=(whole, whole, P(), P(), P(), P(), P()),
        out_specs=(whole, whole, split, split, split, P("gx", ("gy", "gz")), split),
        check_vma=False,
    )
```

profile of v0, /device:TPU:0, one launch (start us, length us, event | category | flops | bytes accessed | tf_op | source)
XLA Modules:
  0.0 84.5 jit_solution(14606102688269683957)
XLA Ops:
  0.6 1.4 %copy.33.refs_3_ = bf16[128,32]{1,0:T(8,128)(2,1)} copy(bf16[128,32]{0,1:T(8,128)(2,1)} %param.12) | data formatting | bytes 16384 | tf_op args[5]
  2.0 0.9 %copy.31 = bf16[32,4,4,128]{3,0,2,1:T(8,128)(2,1)S(1)} copy(bf16[32,4,4,128]{3,2,1,0:T(4,128)(2,1)} %param.7) | data formatting | bytes 262144 | tf_op args[0]
  3.0 0.9 %copy.32 = bf16[32,4,4,128]{3,0,2,1:T(8,128)(2,1)S(1)} copy(bf16[32,4,4,128]{3,2,1,0:T(4,128)(2,1)} %param.8) | data formatting | bytes 262144 | tf_op args[1]
  3.9 0.7 maximum_bitcast_fusion.refs_0_
  4.7 13.9 %halo.1.ext.refs_0_ = bf16[8,8,64,256]{3,2,1,0:T(8,128)(2,1)} custom-call(bf16[4,4,64,128]{3,2,1,0:T(8,128)(2,1)} %maximum_bitcast_fusion.refs_0_), custom_call_target="tpu_custom_call" | custom-call | tf_op jit(solution)/shard_map/halo/pallas_call | solution.py:387
  18.6 11.8 %fine.1 = (f32[6,6,32,256]{3,2,1,0:T(8,128)}, f32[6,6,32,256]{3,2,1,0:T(8,128)}, bf16[16,128]{1,0:T(8,128)(2,1)}) custom-call(bf16[8,8,64,256]{3,2,1,0:T(8,128)(2,1)} %halo.1.ext.refs_0_, bf16[27,32,32]{2,1,0:T(8,128)(2,1)} %refs_5_.1, bf16[27,32,32]{2,1,0:T(8,128)(2,1)} %refs_4_.1), custom_call_target="tpu_custom_call" | custom-call | tf_op jit(solution)/shard_map/fine/pallas_call | solution.py:649
  30.3 13.7 %gather.1 = (bf16[32,16,128]{2,1,0:T(8,128)(2,1)}, bf16[9,384,128]{2,1,0:T(8,128)(2,1)}, bf16[9,384,32]{2,1,0:T(8,128)(2,1)}) custom-call(bf16[16,128]{1,0:T(8,128)(2,1)} %get-tuple-element.22.refs_0_, bf16[9,384,128]{2,1,0:T(8,128)(2,1)} %bitcast.19, bf16[9,96,128]{2,1,0:T(8,128)(2,1)} %bitcast.22), custom_call_target="tpu_custom_call" | custom-call | tf_op jit(solution)/shard_map/gather/pallas_call | solution.py:90
  44.0 13.1 %coarse.1 = (f32[3,3,64,256]{3,2,1,0:T(8,128)}, f32[9,16,96]{2,1,0:T(8,128)}, f32[9,16,24]{2,1,0:T(8,128)}, f32[4,32]{1,0:T(4,128)}) custom-call(bf16[32,16,128]{2,1,0:T(8,128)(2,1)} %get-tuple-element.23.refs_0_, bf16[9,96,128]{2,1,0:T(8,128)(2,1)} %bitcast.23, bf16[9,384,128]{2,1,0:T(8,128)(2,1)} %bitcast.20, bf16[128,32]{1,0:T(8,128)(2,1)} %copy.33.refs_3_, ...), custom_call_target="tpu_custom_call" | custom-call | tf_op jit(solution)/shard_map/coarse/pallas_call | solution.py:684
  57.1 0.0 copy-start.1
  57.1 9.4 %last.1 = (bf16[4,4,32,128]{3,2,1,0:T(8,128)(2,1)}, bf16[4,4,32,128]{3,2,1,0:T(8,128)(2,1)}, bf16[32,8,216]{2,1,0:T(8,128)(2,1)}) custom-call(bf16[8,8,64,256]{3,2,1,0:T(8,128)(2,1)} %halo.1.ext.refs_0_, f32[6,6,32,256]{3,2,1,0:T(8,128)} %get-tuple-element.20.refs_1_, f32[6,6,32,256]{3,2,1,0:T(8,128)} %get-tuple-element.21.refs_2_, ...), custom_call_target="tpu_custom_call" | custom-call | tf_op jit(solution)/shard_map/last/pallas_call | solution.py:704
  66.5 0.0 copy-start
  66.5 1.7 %copy.36 = bf16[32,4,4,128]{3,2,1,0:T(4,128)(2,1)} copy(bf16[32,4,4,128]{3,0,2,1:T(8,128)(2,1)} %bitcast.28) | data formatting | bytes 262144
  68.2 1.6 %copy.37 = bf16[32,4,4,128]{3,2,1,0:T(4,128)(2,1)} copy(bf16[32,4,4,128]{3,0,2,1:T(8,128)(2,1)} %bitcast.27) | data formatting | bytes 262144
  69.8 10.8 %sum_parts.1 = f32[8,216]{1,0:T(8,128)} custom-call(bf16[32,8,216]{2,1,0:T(8,128)(2,1)} %get-tuple-element.29.refs_0_), custom_call_target="tpu_custom_call" | custom-call | tf_op jit(solution)/shard_map/sum_parts/pallas_call | solution.py:90
  80.6 0.0 copy-done.1
  80.6 0.1 copy.34
  80.7 0.8 copy.39
  81.5 0.8 reshape.37
  82.3 0.7 copy.40
  83.0 0.7 copy.38
  83.7 0.0 copy-done
  83.7 0.2 reshape.40
  83.8 0.7 copy.35
  (1 shorter events, 0.0 us)
Async XLA Ops:
  57.1 23.5 %copy-start.1 = (f32[9,16,24]{2,1,0:T(8,128)S(1)}, f32[9,16,24]{2,1,0:T(8,128)}, u32[]{:S(2)}) copy-start(f32[9,16,24]{2,1,0:T(8,128)} %get-tuple-element.30) | copy-start | bytes 41476
  66.5 17.2 %copy-start = (f32[9,16,96]{2,1,0:T(8,128)S(1)}, f32[9,16,96]{2,1,0:T(8,128)}, u32[]{:S(2)}) copy-start(f32[9,16,96]{2,1,0:T(8,128)} %get-tuple-element.31) | copy-start | bytes 165892
where the time goes:
time: 85 us; the launch traced here: 84.5 us
  Pallas kernels  72.6 us (85%)
  local copies, waits for them, and re-layouts  10.5 us (12%)
    pallas_call x2, Pallas kernels, spread_call(): pl.pallas_call(kernel, out_shape=outs, in_specs=vmem(len(args)), out_spec...  24.5 us
    pallas_call x1, Pallas kernels, halo(): pl.pallas_call(lambda *refs: halo_kernel(counts, *refs), out_shape=jax.Sh...  13.9 us
    pallas_call x1, Pallas kernels, shards(): pl.pallas_call(lambda *refs: coarse_kernel(counts, scale, *refs), out_sha...  13.1 us
    pallas_call x1, Pallas kernels, shards(): pl.pallas_call(fine_kernel, out_shape=(field, field, shape((16, 128), bf1...  11.8 us
    pallas_call x1, Pallas kernels, shards(): pl.pallas_call(lambda *refs: last_kernel(counts, *refs), out_shape=(shape...  9.39 us
    unnamed x12, local copies, waits for them, and re-layouts  8.74 us

commit v1 on v0

--- a/solution.py
+++ b/solution.py
@@ -35,8 +35,6 @@
     me = (lax.axis_index("gx") * counts[1] + lax.axis_index("gy")) * counts[2] + lax.axis_index(
         "gz"
     )
-    meet(counts, total, me)
-
     def copy(k):
         peer = (me + k) % total
         return pltpu.make_async_remote_copy(
@@ -83,24 +81,6 @@
 def sum_kernel(counts, scale, x_ref, o_ref, landed, *sems):
     spread_kernel(counts, True, x_ref, landed, *sems, lambda: None)
     o_ref[...] = landed[...].astype(jnp.float32).sum(0) * scale
-
-
-def spread_call(kernel, counts, ident, outs, scratch, name, *args):
-    total = counts[0] * counts[1] * counts[2]
-    return pl.pallas_call(
-        kernel,
-        out_shape=outs,
-        in_specs=vmem(len(args)),
-        out_specs=vmem(len(outs)),
-        scratch_shapes=scratch
-        + [
-            pltpu.SemaphoreType.DMA,
-            pltpu.SemaphoreType.DMA((total,)),
-            pltpu.SemaphoreType.DMA((total,)),
-        ],
-        compiler_params=pltpu.CompilerParams(collective_id=ident, has_side_effects=True),
-        name=name,
-    )(*args)
 
 
 def extended(cells, sides, width):
@@ -293,20 +273,6 @@
         real = (x >= 0) & (x < nx) & (y >= 0) & (y < ny) & (z >= 0) & (z < nz)
         return (x, y, z), real
 
-    rows[...] = jnp.zeros_like(rows)
-    from_low[...] = jnp.zeros_like(from_low)
-    from_high[...] = jnp.zeros_like(from_high)
-    barrier = pltpu.get_barrier_semaphore()
-    met = 0
-    for side in sides:
-        peer, real = there(side, 1)
-        met = met + jnp.where(real, 1, 0)
-
-        @pl.when(real)
-        def _():
-            pl.semaphore_signal(barrier, inc=1, device_id=peer, device_id_type=MESH)
-
-    pl.semaphore_wait(barrier, met)
     d, h = x_ref.shape[:2]
     take = {-1: lambda n: pl.ds(0, 2), 0: lambda n: pl.ds(0, n), 1: lambda n: pl.ds(n - 2, 2)}
     land = {-1: lambda n: pl.ds(n + 2, 2), 0: lambda n: pl.ds(2, n), 1: lambda n: pl.ds(0, 2)}
@@ -381,29 +347,6 @@
 ROOMY = 60 * 1024 * 1024
 
 
-def halo(x, counts, ident):
-    d, h, chans, length = x.shape
-    edge = pltpu.VMEM((chans, 256), jnp.bfloat16)
-    return pl.pallas_call(
-        lambda *refs: halo_kernel(counts, *refs),
-        out_shape=jax.ShapeDtypeStruct((d + 4, h + 4, chans, 256), x.dtype),
-        in_specs=vmem(1),
-        out_specs=vmem(1)[0],
-        scratch_shapes=[
-            pltpu.VMEM((d + 4, h + 4, chans, length), x.dtype),
-            edge,
-            edge,
-            edge,
-            pltpu.SemaphoreType.DMA((10,)),
-            pltpu.SemaphoreType.DMA((10,)),
-        ],
-        compiler_params=pltpu.CompilerParams(
-            collective_id=ident, has_side_effects=True, vmem_limit_bytes=ROOMY
-        ),
-        name="halo",
-    )(x)
-
-
 def stacked(value):
     size = value.shape[1]
     return jnp.concatenate(
@@ -632,6 +575,38 @@
                 ].astype(jnp.bfloat16)
 
 
+def whole_kernel(
+    counts, scale, x_ref, w_in, w_out, w_in9, w_mid9, w_lift,
+    out, g_input, g_mid, g_in, g_lift, sums_out,
+    ext, rows, packed, from_low, from_high, halo_sends, halo_recvs,
+    z_ref, d_ref, mine, taps, total_ref, ws,
+    full, mid_back, in_back, gather_local, gather_sends, gather_recvs,
+    grown, pad_in, pad_mid, pad_smid, pad_sin, table,
+    tj, td, tf, sums, parts, landed, sum_local, sum_sends, sum_recvs,
+):
+    total = counts[0] * counts[1] * counts[2]
+    me = (lax.axis_index("gx") * counts[1] + lax.axis_index("gy")) * counts[2] + lax.axis_index(
+        "gz"
+    )
+    for ref in (rows, from_low, from_high):
+        ref[...] = jnp.zeros_like(ref)
+    meet(counts, total, me)
+    halo_kernel(counts, x_ref, ext, rows, packed, from_low, from_high, halo_sends, halo_recvs)
+    fine_kernel(ext, w_in, w_out, z_ref, d_ref, mine, taps, total_ref, ws)
+    gather_kernel(
+        counts, mine, w_mid9, w_in9, full, mid_back, in_back,
+        gather_local, gather_sends, gather_recvs,
+    )
+    coarse_kernel(
+        counts, scale, full, w_in9, w_mid9, w_lift, mid_back, in_back,
+        grown, g_mid, g_in, g_lift, pad_in, pad_mid, pad_smid, pad_sin, table,
+    )
+    last_kernel(
+        counts, ext, z_ref, d_ref, grown, w_out, w_in, out, g_input, parts, tj, td, tf, sums, ws
+    )
+    sum_kernel(counts, scale, parts, sums_out, landed, sum_local, sum_sends, sum_recvs)
+
+
 def shards(features, cotangent, w_fine_in, w_coarse_in, w_coarse_mid, w_lift, w_fine_out):
     counts = tuple(lax.axis_size(axis) for axis in AXES)
     nx, ny, nz = counts
@@ -641,94 +616,60 @@
     scale = 1.0 / math.sqrt(total * depth * height * length)
     f32, bf16 = jnp.float32, jnp.bfloat16
     shape = jax.ShapeDtypeStruct
-    params = pltpu.CompilerParams(vmem_limit_bytes=ROOMY)
-
     rows = jnp.concatenate([features, cotangent]).transpose(1, 2, 0, 3)
-    ext = halo(rows, counts, 2)
-    field = shape((6, 6, chans, 256), f32)
-    z_first, d_joined, mine = pl.pallas_call(
-        fine_kernel,
-        out_shape=(field, field, shape((16, 128), bf16)),
-        in_specs=vmem(3),
-        out_specs=vmem(3),
+    co, cw = wide // (ny * nz), wide // nx
+    ci = chans // nx
+    pads = [3 * chans, 3 * wide, 3 * cw, 3 * ci]
+    block = (2 * chans // (ny * nz), 27 * ci)
+    edge = pltpu.VMEM((2 * chans, 256), bf16)
+    near = pltpu.VMEM((6, 6, 3 * chans, 128), bf16)
+    field = pltpu.VMEM((6, 6, chans, 256), f32)
+    one, many = pltpu.SemaphoreType.DMA, pltpu.SemaphoreType.DMA((total,))
+    output, grad_input, g_mid, g_in, g_lift, sums = pl.pallas_call(
+        lambda *refs: whole_kernel(counts, scale, *refs),
+        out_shape=(
+            shape((4, 4, chans, 128), bf16),
+            shape((4, 4, chans, 128), bf16),
+            shape((9, co, 3 * cw), f32),
+            shape((9, co, 3 * ci), f32),
+            shape((chans // (ny * nz), cw), f32),
+            shape(block, f32),
+        ),
+        in_specs=vmem(6),
+        out_specs=vmem(6),
         scratch_shapes=[
+            pltpu.VMEM((8, 8, 2 * chans, 256), bf16),
+            pltpu.VMEM((8, 8, 2 * chans, 128), bf16),
+            edge, edge, edge,
+            pltpu.SemaphoreType.DMA((10,)),
+            pltpu.SemaphoreType.DMA((10,)),
+            field, field,
+            pltpu.VMEM((16, 128), bf16),
             pltpu.VMEM((8, 8, 192, 256), bf16),
             pltpu.VMEM((64, 128), f32),
             pltpu.VMEM((2, chans, 27 * chans), bf16),
+            pltpu.VMEM((total, 16, 128), bf16),
+            pltpu.VMEM((9, 3 * wide, wide), bf16),
+            pltpu.VMEM((9, 3 * wide, chans), bf16),
+            one, many, many,
+            pltpu.VMEM((3, 3, 2 * chans, 256), f32),
+        ]
+        + [pltpu.VMEM((nx + 2, ny + 2, 128, k), bf16) for k in pads]
+        + [
+            pltpu.VMEM((nx, ny, 128, 2 * chans), bf16),
+            near, near, near,
+            pltpu.VMEM((2, 27 * chans, chans), f32),
+            pltpu.VMEM((total,) + block, bf16),
+            pltpu.VMEM((total,) + block, bf16),
+            one, many, many,
         ],
-        compiler_params=params,
-        name="fine",
-    )(ext, w_fine_in, w_fine_out)
-
-    w_in9 = w_coarse_in.reshape(9, 3 * chans, wide)
-    w_mid9 = w_coarse_mid.reshape(9, 3 * wide, wide)
-    full, mid_back, in_back = spread_call(
-        lambda *refs: gather_kernel(counts, *refs),
-        counts,
-        0,
-        (
-            shape((total,) + mine.shape, bf16),
-            shape(w_mid9.shape, bf16),
-            shape((9, 3 * wide, chans), bf16),
+        compiler_params=pltpu.CompilerParams(
+            collective_id=0, has_side_effects=True, vmem_limit_bytes=ROOMY
         ),
-        [],
-        "gather",
-        mine,
-        w_mid9,
-        w_in9,
-    )
-
-    co, cw = wide // (ny * nz), wide // nx
-    ci = chans // nx
-    pads = [3 * chans, 3 * wide, 3 * cw, 3 * ci]
-    grown, g_mid, g_in, g_lift = pl.pallas_call(
-        lambda *refs: coarse_kernel(counts, scale, *refs),
-        out_shape=(
-            shape((3, 3, 2 * chans, 256), f32),
-            shape((9, co, 3 * cw), f32),
-            shape((9, co, 3 * ci), f32),
-            shape((chans // (ny * nz), cw), f32),
-        ),
-        in_specs=vmem(6),
-        out_specs=vmem(4),
-        scratch_shapes=[pltpu.VMEM((nx + 2, ny + 2, 128, k), bf16) for k in pads]
-        + [pltpu.VMEM((nx, ny, 128, 2 * chans), bf16)],
-        compiler_params=params,
-        name="coarse",
+        name="whole",
     )(
-        full, w_in9, w_mid9, w_lift, mid_back, in_back
-    )
-
-    near = pltpu.VMEM((6, 6, 3 * chans, 128), bf16)
-    block = (2 * chans // (ny * nz), 27 * ci)
-    output, grad_input, parts = pl.pallas_call(
-        lambda *refs: last_kernel(counts, *refs),
-        out_shape=(
-            shape((4, 4, chans, 128), bf16),
-            shape((4, 4, chans, 128), bf16),
-            shape((total,) + block, bf16),
-        ),
-        in_specs=vmem(6),
-        out_specs=vmem(3),
-        scratch_shapes=[
-            near,
-            near,
-            near,
-            pltpu.VMEM((2, 27 * chans, chans), f32),
-            pltpu.VMEM((2, chans, 27 * chans), bf16),
-        ],
-        compiler_params=params,
-        name="last",
-    )(ext, z_first, d_joined, grown, w_fine_out, w_fine_in)
-
-    (sums,) = spread_call(
-        lambda *refs: sum_kernel(counts, scale, *refs),
-        counts,
-        1,
-        (shape(block, f32),),
-        [pltpu.VMEM((total,) + block, bf16)],
-        "sum_parts",
-        parts,
+        rows, w_fine_in, w_fine_out,
+        w_coarse_in.reshape(9, 3 * chans, wide), w_coarse_mid.reshape(9, 3 * wide, wide), w_lift,
     )
     sums = sums.reshape(2, -1, 27, ci).transpose(0, 2, 3, 1)
 

time: 85 us -> 66.8 us (0.79)
  Pallas kernels: 72.6 us -> 56.3 us
  local copies, waits for them, and re-layouts: 10.5 us -> 8.77 us
    pallas_call x6 -> x1, Pallas kernels: 72.6 us -> 56.3 us  [shards(): pl.pallas_call(lambda *refs: whole_kernel(counts, scale, *refs), out_shap...]
    unnamed x12 -> x21, local copies, waits for them, and re-layouts: 8.74 us -> 7.72 us
where the time goes in v1:
time: 66.8 us; the launch traced here: 66.5 us
  Pallas kernels  56.3 us (84%)
  local copies, waits for them, and re-layouts  8.77 us (13%)
  other arithmetic  0.73 us (1%)
  between operations  0.73 us (1%)
    pallas_call x1, Pallas kernels, shards(): pl.pallas_call(lambda *refs: whole_kernel(counts, scale, *refs), out_shap...  56.3 us
    unnamed x21, local copies, waits for them, and re-layouts  7.72 us

profile of v1, /device:TPU:0, one launch (start us, length us, event | category | flops | bytes accessed | tf_op | source)
XLA Modules:
  0.0 66.5 jit_solution(13635049590750759161)
XLA Ops:
  0.6 1.4 %copy.33.refs_5_ = bf16[128,32]{1,0:T(8,128)(2,1)} copy(bf16[128,32]{0,1:T(8,128)(2,1)} %param.12) | data formatting | bytes 16384 | tf_op args[5]
  2.0 1.0 %copy.31 = bf16[32,4,4,128]{3,0,2,1:T(8,128)(2,1)S(1)} copy(bf16[32,4,4,128]{3,2,1,0:T(4,128)(2,1)} %param.7) | data formatting | bytes 262144 | tf_op args[0]
  3.0 0.0 copy-done
  3.1 0.7 %maximum_bitcast_fusion.refs_0_ = bf16[4,4,64,128]{3,2,1,0:T(8,128)(2,1)} fusion(bf16[32,4,4,128]{3,0,2,1:T(8,128)(2,1)S(1)} %copy.32, bf16[32,4,4,128]{3,0,2,1:T(8,128)(2,1)S(1)} %copy.31), kind=kLoop, calls=%fused_computation | loop fusion | flops 524288 | bytes 524288 | tf_op jit(solution)/shard_map/transpose | solution.py:619
  3.8 56.3 %whole.1 = (bf16[4,4,32,128]{3,2,1,0:T(8,128)(2,1)}, bf16[4,4,32,128]{3,2,1,0:T(8,128)(2,1)}, f32[9,16,96]{2,1,0:T(8,128)}, f32[9,16,24]{2,1,0:T(8,128)}, f32[4,32]{1,0:T(4,128)}, /*index=5*/f32[8,216]{1,0:T(8,128)}) custom-call(bf16[4,4,64,128]{3,2,1,0:T(8,128)(2,1)} %maximum_bitcast_fusion.refs_0_, bf16[27,32,32]{2,1,0:T(8,128)(2,1)} %refs_1_.1, ...), custom_call_target="tpu_custom_call" | custom-call | tf_op jit(solution)/shard_map/whole/pallas_call | solution.py:628
  60.1 0.0 copy-start.1
  60.1 1.7 %copy.36 = bf16[32,4,4,128]{3,2,1,0:T(4,128)(2,1)} copy(bf16[32,4,4,128]{3,0,2,1:T(8,128)(2,1)} %bitcast.26) | data formatting | bytes 262144
  61.8 0.0 copy-done.1
  61.8 0.7 %copy.37 = bf16[32,4,4,128]{3,2,1,0:T(4,128)(2,1)} copy(bf16[32,4,4,128]{3,0,2,1:T(8,128)(2,1)S(1)} %bitcast.25) | data formatting | bytes 262144
  62.5 0.2 copy-done.3
  62.7 0.1 copy.34
  62.7 0.0 copy-start.4
  62.8 0.8 %copy.39 = f32[27,8,16]{0,2,1:T(8,128)} copy(f32[27,8,16]{2,1,0:T(8,128)S(1)} %bitcast.22) | data formatting | bytes 27648
  63.5 0.0 copy-done.4
  63.5 0.1 reshape.37
  63.6 0.0 copy-start.2
  63.6 0.7 %copy.40 = f32[27,8,4]{0,2,1:T(4,128)} copy(f32[27,8,4]{1,0,2:T(8,128)S(1)} %get-tuple-element.40) | data formatting | bytes 6912
  64.3 0.7 %copy.38 = f32[27,8,4]{0,2,1:T(4,128)} copy(f32[27,8,4]{1,0,2:T(8,128)S(1)} %get-tuple-element.41) | data formatting | bytes 6912
  65.0 0.0 copy-done.2
  65.0 0.2 reshape.40
  65.2 0.0 copy-start.5
  65.2 0.7 %copy.35 = f32[9,3,32,16]{2,3,1,0:T(8,128)} copy(f32[9,3,32,16]{2,1,3,0:T(4,128)S(1)} %bitcast.19) | data formatting | bytes 110592 | tf_op jit(solution)/shard_map/transpose | solution.py:677
  65.9 0.0 copy-done.5
  65.9 0.6 copy.42
  (4 shorter events, 0.1 us)
Async XLA Ops:
  2.0 1.0 %copy-start = (bf16[32,4,4,128]{3,2,1,0:T(4,128)(2,1)S(1)}, bf16[32,4,4,128]{3,2,1,0:T(4,128)(2,1)}, u32[]{:S(2)}) copy-start(bf16[32,4,4,128]{3,2,1,0:T(4,128)(2,1)} %param.8) | copy-start | bytes 393220
  60.1 1.7 %copy-start.1 = (bf16[4,4,32,128]{3,2,1,0:T(8,128)(2,1)S(1)}, bf16[4,4,32,128]{3,2,1,0:T(8,128)(2,1)}, u32[]{:S(2)}) copy-start(bf16[4,4,32,128]{3,2,1,0:T(8,128)(2,1)} %get-tuple-element.14) | copy-start | bytes 393220
  61.8 0.9 %copy-start.3 = (f32[9,16,24]{2,1,0:T(8,128)S(1)}, f32[9,16,24]{2,1,0:T(8,128)}, u32[]{:S(2)}) copy-start(f32[9,16,24]{2,1,0:T(8,128)} %get-tuple-element.16) | copy-start | bytes 41476
  62.7 0.8 %copy-start.4 = (f32[8,216]{1,0:T(8,128)S(1)}, f32[8,216]{1,0:T(8,128)}, u32[]{:S(2)}) copy-start(f32[8,216]{1,0:T(8,128)} %get-tuple-element.15) | copy-start | bytes 20740
  63.6 1.4 %copy-start.2 = (f32[9,16,96]{2,1,0:T(8,128)S(1)}, f32[9,16,96]{2,1,0:T(8,128)}, u32[]{:S(2)}) copy-start(f32[9,16,96]{2,1,0:T(8,128)} %get-tuple-element.17) | copy-start | bytes 165892
  65.2 0.7 %copy-start.5 = (f32[4,32]{1,0:T(4,128)S(1)}, f32[4,32]{1,0:T(4,128)}, u32[]{:S(2)}) copy-start(f32[4,32]{1,0:T(4,128)} %get-tuple-element.18) | copy-start | bytes 1540

commit v2 on v1

v2 whole, which is shorter than its diff:
```python
import math

import jax
import jax.numpy as jnp
from jax import lax
from jax.experimental import pallas as pl
from jax.experimental.pallas import tpu as pltpu
from jax.sharding import PartitionSpec as P

AXES = ("gx", "gy", "gz")
MESH = pl.DeviceIdType.MESH
DIRECT = 64


def place(flat, counts):
    nx, ny, nz = counts
    return (flat // (ny * nz), (flat // nz) % ny, flat % nz)


def extended(cells, sides, width):
    for axis, dim in sides:
        count = lax.axis_size(axis)
        ends = count - 1
        head = lax.slice_in_dim(cells, 0, width, axis=dim)
        tail = lax.slice_in_dim(cells, cells.shape[dim] - width, cells.shape[dim], axis=dim)
        cells = jnp.concatenate(
            [
                lax.ppermute(tail, axis, [(i, (i + 1) % count) for i in range(ends)]),
                cells,
                lax.ppermute(head, axis, [((i + 1) % count, i) for i in range(ends)]),
            ],
            axis=dim,
        )
    return cells


def silu_slope(values):
    sigma = jax.nn.sigmoid(values)
    return sigma * (1.0 + values * (1.0 - sigma))


def conv_valid(padded, weight, form="NCDHW"):
    kernel = weight.reshape(3, 3, 3, weight.shape[1], weight.shape[2])
    result = lax.conv_general_dilated(
        padded[None],
        kernel,
        (1, 1, 1),
        "VALID",
        dimension_numbers=(form, "DHWIO", form),
        preferred_element_type=jnp.float32,
    )
    return result[0]


def flipped(weight):
    return jnp.flip(weight, 0).transpose(0, 2, 1)


def pool_blocks(field):
    chans, depth, height, length = field.shape
    grouped = field.astype(jnp.float32).reshape(
        chans, depth // 4, 4, height // 4, 4, length // 4, 4
    )
    return grouped.sum(axis=(2, 4, 6))


def spread_up(field):
    chans, depth, height, length = field.shape
    grown = jnp.broadcast_to(
        field[:, :, None, :, None, :, None], (chans, depth, 4, height, 4, length, 4)
    )
    return grown.reshape(chans, depth * 4, height * 4, length * 4)


def tap_grad_direct(padded, grad):
    depth = padded.shape[1] - 2
    height = padded.shape[2] - 2
    length = padded.shape[3] - 2
    flat_grad = grad.reshape(grad.shape[0], -1)
    blocks = []
    for tap in range(27):
        shift_x, shift_y, shift_z = (tap // 9, tap // 3 % 3, tap % 3)
        window = padded[
            :, shift_x : shift_x + depth, shift_y : shift_y + height, shift_z : shift_z + length
        ].reshape(padded.shape[0], -1)
        blocks.append(
            lax.dot_general(
                window, flat_grad, (((1,), (1,)), ((), ())), preferred_element_type=jnp.float32
            )
        )
    return jnp.stack(blocks)


def fine_rim(field):
    return extended(field, (("gx", 1), ("gy", 2), ("gz", 3)), 1)


def coarse_rim(field):
    return extended(field, (("gx", 1), ("gy", 2), ("gz", 3)), 1)


def reduce_grad(partial_value):
    first = lax.psum_scatter(partial_value, "gx", scatter_dimension=1, tiled=True)
    return lax.psum_scatter(first, ("gy", "gz"), scatter_dimension=2, tiled=True)


def input_share(field):
    parts = lax.all_to_all(field[None], "gx", split_axis=1, concat_axis=0, tiled=True)
    moved = jnp.moveaxis(parts, 0, 1)
    moved = moved.reshape(moved.shape[0], -1, moved.shape[3], moved.shape[4])
    moved = lax.all_gather(moved, "gy", axis=2, tiled=True)
    return lax.all_gather(moved, "gz", axis=3, tiled=True)


def output_share(field):
    parts = lax.all_to_all(field[None], ("gy", "gz"), split_axis=1, concat_axis=0, tiled=True)
    count_y = lax.axis_size("gy")
    count_z = lax.axis_size("gz")
    chans = parts.shape[1]
    depth, height, length = (parts.shape[2], parts.shape[3], parts.shape[4])
    grid = parts.reshape(count_y, count_z, chans, depth, height, length).transpose(2, 3, 0, 4, 1, 5)
    grid = grid.reshape(chans, depth, count_y * height, count_z * length)
    return lax.all_gather(grid, "gx", axis=1, tiled=True)


def shards_layered(features, cotangent, w_fine_in, w_coarse_in, w_coarse_mid, w_lift, w_fine_out):
    depth, height, length = (features.shape[1], features.shape[2], features.shape[3])
    whole_cells = (
        depth * lax.axis_size("gx") * height * lax.axis_size("gy") * length * lax.axis_size("gz")
    )
    scale = 1.0 / math.sqrt(whole_cells)
    padded_in = fine_rim(features)
    z_first = conv_valid(padded_in, w_fine_in)
    act_first = jax.nn.silu(z_first).astype(jnp.bfloat16)
    pooled = (pool_blocks(act_first) / 64.0).astype(jnp.bfloat16)
    pooled_pad = coarse_rim(pooled)
    z_second = conv_valid(pooled_pad, w_coarse_in)
    act_second = jax.nn.silu(z_second).astype(jnp.bfloat16)
    second_pad = coarse_rim(act_second)
    z_third = conv_valid(second_pad, w_coarse_mid)
    act_third = jax.nn.silu(z_third).astype(jnp.bfloat16)
    lifted = lax.dot_general(
        w_lift, act_third, (((0,), (0,)), ((), ())), preferred_element_type=jnp.float32
    )
    joined = (act_first.astype(jnp.float32) + spread_up(lifted)).astype(jnp.bfloat16)
    padded_joined = fine_rim(joined)
    output = conv_valid(padded_joined, w_fine_out).astype(jnp.bfloat16)
    part_fine_out = tap_grad_direct(padded_joined, cotangent) * scale
    d_joined = conv_valid(fine_rim(cotangent), flipped(w_fine_out))
    d_lift = pool_blocks(d_joined)
    lift_partial = (
        lax.dot_general(
            act_third.astype(jnp.float32),
            d_lift,
            (((1, 2, 3), (1, 2, 3)), ((), ())),
            precision=lax.Precision.HIGHEST,
        )
        * scale
    )
    d_third = lax.dot_general(
        w_lift.astype(jnp.float32),
        d_lift,
        (((1,), (0,)), ((), ())),
        precision=lax.Precision.HIGHEST,
    )
    dz_third = (d_third * silu_slope(z_third)).astype(jnp.bfloat16)
    dz_third_pad = coarse_rim(dz_third)
    grad_coarse_mid = None
    sources = input_share(act_second)
    sources_pad = jnp.pad(sources, ((0, 0), (1, 1), (1, 1), (1, 1)))
    targets = output_share(dz_third)
    grad_coarse_mid = tap_grad_direct(sources_pad, targets) * scale
    dz_second = (conv_valid(dz_third_pad, flipped(w_coarse_mid)) * silu_slope(z_second)).astype(
        jnp.bfloat16
    )
    dz_second_pad = coarse_rim(dz_second)
    part_coarse_in = tap_grad_direct(pooled_pad, dz_second) * scale
    d_pool = conv_valid(dz_second_pad, flipped(w_coarse_in))
    dz_first = ((d_joined + spread_up(d_pool) / 64.0) * silu_slope(z_first)).astype(jnp.bfloat16)
    part_fine_in = tap_grad_direct(padded_in, dz_first) * scale
    grad_input = conv_valid(fine_rim(dz_first), flipped(w_fine_in)).astype(jnp.bfloat16)
    pending = [part_fine_out, lift_partial[None], part_coarse_in, part_fine_in]
    reduced = [reduce_grad(partial_value) for partial_value in pending]
    grad_fine_out = reduced[0]
    grad_lift = reduced[1][0]
    grad_coarse_in = reduced[2]
    grad_fine_in = reduced[3]
    return (
        output,
        grad_input,
        grad_fine_in,
        grad_coarse_in,
        grad_coarse_mid,
        grad_lift,
        grad_fine_out,
    )


SIDES = [(i, j, 0) for i in (-1, 0, 1) for j in (-1, 0, 1) if (i, j) != (0, 0)]
SIDES += [(i, j, k) for i in (-1, 0, 1) for j in (-1, 0, 1) for k in (-1, 1)]
ROOMY = 60 * 1024 * 1024


def vmem(count):
    return [pl.BlockSpec(memory_space=pltpu.VMEM)] * count


def slot(i, j, k):
    return ((i + 1) * 3 + j + 1) * 2 + (1 if k > 0 else 0)


def there(counts, side, sign):
    place_of = [lax.axis_index(axis) + sign * step for axis, step in zip(AXES, side)]
    real = True
    for at, count, step in zip(place_of, counts, side):
        if step != 0:
            real = real & (at >= 0) & (at < count)
    return tuple(place_of), real


def swap_copy(counts, n, rows, packed, got, sends, recvs):
    i, j, k = SIDES[n]
    take = {-1: pl.ds(1, 1), 0: pl.ds(1, 4), 1: pl.ds(4, 1)}
    land = {-1: pl.ds(5, 1), 0: pl.ds(1, 4), 1: pl.ds(0, 1)}
    if k == 0:
        source, target = rows.at[take[i], take[j]], rows.at[land[i], land[j]]
    else:
        source, target = packed, got.at[slot(-i, -j, -k)]
    return pltpu.make_async_remote_copy(
        src_ref=source,
        dst_ref=target,
        send_sem=sends.at[n],
        recv_sem=recvs.at[n],
        device_id=there(counts, SIDES[n], 1)[0],
        device_id_type=MESH,
    )


def swap_start(counts, *refs):
    for n in range(len(SIDES)):

        @pl.when(there(counts, SIDES[n], 1)[1])
        def _():
            swap_copy(counts, n, *refs).start()


def swap_finish(counts, *refs):
    for n in range(len(SIDES)):

        @pl.when(there(counts, SIDES[n], -1)[1])
        def _():
            swap_copy(counts, n, *refs).wait_recv()

        @pl.when(there(counts, SIDES[n], 1)[1])
        def _():
            swap_copy(counts, n, *refs).wait_send()


def spot(x, y):
    return (x + 1) * 6 + y + 1


def lanes_of(rows, width=128):
    return lax.broadcasted_iota(jnp.int32, (rows, width), 1)


def clear_rim(rows, got):
    rows[0] = jnp.zeros(rows.shape[1:], rows.dtype)
    rows[5] = jnp.zeros(rows.shape[1:], rows.dtype)
    for x in range(1, 5):
        rows[x, 0] = jnp.zeros(rows.shape[2:], rows.dtype)
        rows[x, 5] = jnp.zeros(rows.shape[2:], rows.dtype)
    got[...] = jnp.zeros_like(got)


def edges(values, x, y, group):
    lane = lanes_of(32)
    place_of = spot(x, y)
    for f, value in enumerate(values):
        turned = pltpu.roll(value, (2 * place_of + 1 + 64 * f) % 128, 1)
        group = jnp.where(lane // 2 == place_of + 32 * f, turned, group)
    return group


def columns(got, f):
    lane = lanes_of(32)
    low = lane % 2 == 1
    at_x, at_y = lane // 12, lane // 2 % 6
    result = jnp.zeros((32, 128), jnp.float32)
    for i in (-1, 0, 1):
        for j in (-1, 0, 1):
            mine = (lane < 72) & (at_x == 0 if i < 0 else at_x == 5 if i > 0 else (at_x > 0) & (at_x < 5))
            mine = mine & (at_y == 0 if j < 0 else at_y == 5 if j > 0 else (at_y > 0) & (at_y < 5))
            for k in (-1, 1):
                turn = (48 * i + 8 * j - 64 * f - k) % 128
                block = pltpu.roll(got[slot(i, j, k)].astype(jnp.float32), turn, 1)
                result = jnp.where(mine & (low if k < 0 else ~low), block, result)
    return result


def column_window(value):
    return jnp.concatenate(
        [
            pltpu.roll(value, (-12 * (a - 1) - 2 * (b - 1)) % 128, 1)
            for a in range(3)
            for b in range(3)
        ]
    ).astype(jnp.bfloat16)


def dot(a, b):
    return jnp.dot(a, b, preferred_element_type=jnp.float32)


def dot_over(a, b, dims, precision=None):
    return lax.dot_general(
        a, b, ((dims[:1], dims[1:]), ((), ())), precision=precision, preferred_element_type=jnp.float32
    )


def ahead(weight):
    size = weight.shape[1]
    taps = weight[...].reshape(9, 3, size, weight.shape[2])
    return jnp.concatenate([taps[:, c].reshape(9 * size, weight.shape[2]).T for c in range(3)])


def back(weight):
    return jnp.concatenate(
        [
            jnp.concatenate([weight[26 - 3 * ab - c] for ab in range(9)], axis=1)
            for c in range(3)
        ]
    )


def near(ref, x, chans):
    return jnp.concatenate(
        [
            jnp.concatenate([ref[x + a, y + b, chans, :] for y in range(4)], axis=1)
            for a in range(3)
            for b in range(3)
        ]
    )


def settle(taps, rim, x):
    lane = lanes_of(32)
    rows = []
    for y in range(4):
        part = taps[:, y * 128 : y * 128 + 128]
        edge = pltpu.roll(rim, (127 - 2 * spot(x, y)) % 128, 1)
        low = jnp.where(lane == 0, edge, pltpu.roll(part[:32], 1, 1))
        high = jnp.where(lane == 127, edge, pltpu.roll(part[64:], 127, 1))
        rows.append(low + part[32:64] + high)
    return rows


def rim_of(weight, window):
    taps = dot(weight, window)
    return jnp.where(lanes_of(32) % 2 == 1, taps[:32], taps[64:])


def thrice(value):
    lane = lax.broadcasted_iota(jnp.int32, value.shape, 1) % 128
    size = value.shape[1]
    value = value.astype(jnp.float32)
    parts = []
    for at in range(0, size, 128):
        part = value[:, at : at + 128]
        spare = lane[:, :128]
        parts.append(
            jnp.concatenate(
                [
                    jnp.where(spare == 127, 0.0, pltpu.roll(part, 127, 1)),
                    part,
                    jnp.where(spare == 0, 0.0, pltpu.roll(part, 1, 1)),
                ]
            )
        )
    return jnp.concatenate(parts, axis=1).astype(jnp.bfloat16)


def thrice_rim(edge):
    low = lanes_of(32) % 2 == 1
    return jnp.concatenate(
        [jnp.where(low, edge, 0.0), jnp.zeros_like(edge), jnp.where(low, 0.0, edge)]
    ).astype(jnp.bfloat16)


def silu_parts(z):
    sigma = jax.nn.sigmoid(z)
    act = (z * sigma).astype(jnp.bfloat16).astype(jnp.float32)
    return act, sigma * (1.0 + z * (1.0 - sigma))


def spread(value, chooser):
    high = value.astype(jnp.bfloat16)
    rest = value - high.astype(jnp.float32)
    middle = rest.astype(jnp.bfloat16)
    low = (rest - middle.astype(jnp.float32)).astype(jnp.bfloat16)
    count = value.shape[0]
    chosen = dot(jnp.concatenate([high, middle, low]), chooser)
    return chosen[:count] + chosen[count : 2 * count] + chosen[2 * count :]


def chooser_of(blocks, step, inner):
    row = lax.broadcasted_iota(jnp.int32, (27 * blocks, 128 * blocks), 0)
    lane = lax.broadcasted_iota(jnp.int32, (27 * blocks, 128 * blocks), 1)
    tap = lane % 128
    ab, c = tap // 3, tap % 3
    source = ab * step + c * inner + lane // 128
    return jnp.where((row == source) & (tap < 27), 1.0, 0.0).astype(jnp.bfloat16)


def whole_kernel(
    counts, scale, fea, cot, w_in, w_out, w_in9, w_mid9, w_lift,
    out, g_input, g_fine_in, g_in, g_mid, g_lift, g_fine_out,
    one, two, got_one, got_two, pack_one, pack_two, sends_one, recvs_one, sends_two, recvs_two,
    tmp, ws, near_rim, rim_sums, total_ref, mine, full, mid_back, in_back, weight_sems,
    w9, wm9, gather_local, gather_sends, gather_recvs,
    grown, grown_rim, pad_in, pad_mid, pad_smid, pad_sin, table, thirds,
    jd, dz_edges, sums, parts, landed, sum_local, sum_sends, sum_recvs,
):
    nx, ny, nz = counts
    total = nx * ny * nz
    gx, gy, gz = (lax.axis_index(axis) for axis in AXES)
    me = (gx * ny + gy) * nz + gz
    f32, bf16 = jnp.float32, jnp.bfloat16
    fetches = [
        pltpu.make_async_copy(w_in9, w9, weight_sems.at[0]),
        pltpu.make_async_copy(w_mid9, wm9, weight_sems.at[1]),
    ]
    for fetch in fetches:
        fetch.start()
    clear_rim(one, got_one)
    clear_rim(two, got_two)
    barrier = pltpu.get_barrier_semaphore()

    def greet(k, carry):
        pl.semaphore_signal(
            barrier, inc=1, device_id=place((me + k) % total, counts), device_id_type=MESH
        )
        return carry

    lax.fori_loop(1, total, greet, 0)

    group = jnp.zeros((32, 128), f32)
    for x in range(4):
        tmp[0] = fea[:, x].astype(f32).reshape(128, 128)
        tmp[1] = cot[:, x].astype(f32).reshape(128, 128)
        for y in range(4):
            values = [tmp[f, pl.ds(y, 32, stride=4), :] for f in range(2)]
            one[x + 1, y + 1] = jnp.concatenate(values).astype(bf16)
            group = edges(values, x, y, group)
    pack_one[...] = group.astype(bf16)
    ws[0], ws[1], ws[2], ws[3] = ahead(w_in), back(w_out), ahead(w_out), back(w_in)
    pl.semaphore_wait(barrier, total - 1)
    first = (counts, one, pack_one, got_one, sends_one, recvs_one)
    swap_start(*first)
    swap_finish(*first)

    for f in range(2):
        window = column_window(columns(got_one, f))
        if f == 0:
            near_rim[0] = window
        rim_sums[f] = rim_of(ws[f], window)
    total_ref[...] = jnp.zeros_like(total_ref)
    pack_two[...] = jnp.zeros_like(pack_two)

    def fine(x, carry):
        z = settle(dot(ws[0], near(one, x, slice(0, 32))), rim_sums[0], x)
        d = settle(dot(ws[1], near(one, x, slice(32, 64))), rim_sums[1], x)
        group = pack_two[...].astype(f32)
        acts = jnp.zeros((32, 128), f32)
        for y in range(4):
            two[x + 1, y + 1] = jnp.concatenate([z[y], d[y]]).astype(bf16)
            group = edges([z[y], d[y]], x, y, group)
            acts = acts + silu_parts(z[y])[0]
        pack_two[...] = group.astype(bf16)
        total_ref[...] += jnp.concatenate([acts, d[0] + d[1] + d[2] + d[3]])
        return carry

    lax.fori_loop(0, 4, fine, 0)
    row = lax.broadcasted_iota(jnp.int32, (32, 128), 0)
    pick_cell = jnp.where(lanes_of(32) // 4 == row, 1.0, 0.0)
    means = dot_over(pick_cell, total_ref[...], (1, 1), lax.Precision.HIGHEST)
    both = jnp.concatenate([means[:, :32] * (1.0 / 64.0), means[:, 32:]], axis=1)
    mine[...] = jnp.concatenate([both[:16], both[16:]], axis=1).astype(bf16)

    def spread_copy(k, source, target, local_sems):
        peer = (me + k) % total
        return pltpu.make_async_remote_copy(
            src_ref=source(peer),
            dst_ref=target.at[me],
            send_sem=local_sems[0].at[k],
            recv_sem=local_sems[1].at[k],
            device_id=place(peer, counts),
            device_id_type=MESH,
        )

    def gather_copy(k):
        return spread_copy(k, lambda peer: mine, full, (gather_sends, gather_recvs))

    def sum_copy(k):
        return spread_copy(k, lambda peer: parts.at[peer], landed, (sum_sends, sum_recvs))

    def each_peer(act):
        def step(k, carry):
            act(k)
            return carry

        lax.fori_loop(1, total, step, 0)

    each_peer(lambda k: gather_copy(k).start())
    own = pltpu.make_async_copy(mine, full.at[me], gather_local)
    own.start()
    second = (counts, two, pack_two, got_two, sends_two, recvs_two)
    swap_start(*second)

    for fetch in fetches:
        fetch.wait()
    wide, narrow = w9.shape[2], in_back.shape[2]

    def turn(ab, carry):
        for c in range(3):
            rows = slice(c * wide, c * wide + wide)
            mid_back[ab, rows, :] = wm9[8 - ab, (2 - c) * wide : (3 - c) * wide, :].T
            in_back[ab, rows, :] = w9[8 - ab, (2 - c) * narrow : (3 - c) * narrow, :].T
        return carry

    lax.fori_loop(0, 9, turn, 0)
    for pad in (pad_in, pad_mid, pad_smid, pad_sin):
        pad[...] = jnp.zeros_like(pad)
    own.wait()
    each_peer(lambda k: gather_copy(k).wait())

    cells = nx * ny * 128

    def pick(size, pieces, index):
        each = size // pieces
        row = lax.broadcasted_iota(jnp.int32, (size, each), 0)
        column = lax.broadcasted_iota(jnp.int32, (size, each), 1)
        return jnp.where(row == index * each + column, 1.0, 0.0).astype(bf16)

    at_o = gy * nz + gz
    pick_mid, pick_in = pick(128, nx, gx), pick(32, nx, gx)
    pick_o, pick_lift = pick(128, ny * nz, at_o), pick(32, ny * nz, at_o)

    def fill(pad, value):
        at = lax.broadcasted_iota(jnp.int32, value.shape, 0) % 128
        low = jnp.where(at == 0, 0.0, pltpu.roll(value, 1, 0))
        high = jnp.where(at == 127, 0.0, pltpu.roll(value, cells - 1, 0))
        wide = jnp.concatenate([low, value, high], axis=1).astype(bf16)
        pad[1 : nx + 1, 1 : ny + 1] = wide.reshape(nx, ny, 128, wide.shape[1])

    def window(pad, ab):
        a, b = ab // 3, ab % 3
        return pad[a : a + nx, b : b + ny].reshape(cells, pad.shape[3])

    def conv(pad, weight):
        result = dot(window(pad, 0), weight[0])
        for ab in range(1, 9):
            result = result + dot(window(pad, ab), weight[ab])
        return result

    def slope(v):
        sigma = jax.nn.sigmoid(v)
        return sigma * (1.0 + v * (1.0 - sigma))

    pieces = []
    for k in range(nx * ny):
        for z in range(nz):
            block = full[k * nz + z]
            pieces += [block[:, :64], block[:, 64:]]
    both = jnp.concatenate(pieces)
    pooled, d_lift = both[:, :32], both[:, 32:]
    fill(pad_in, pooled.astype(f32))
    z_second = conv(pad_in, w9)
    act_second = jax.nn.silu(z_second)
    fill(pad_mid, act_second)
    z_third = conv(pad_mid, wm9)
    act_third = jax.nn.silu(z_third).astype(bf16)
    lifted = dot(act_third, w_lift[...].T)
    dz_third = (dot(d_lift, w_lift[...]) * slope(z_third)).astype(bf16)
    fill(pad_mid, dz_third.astype(f32))
    dz_second = (conv(pad_mid, mid_back) * slope(z_second)).astype(bf16)
    fill(pad_mid, dz_second.astype(f32))
    d_pool = conv(pad_mid, in_back)
    table[...] = (
        jnp.concatenate([lifted, d_pool * (1.0 / 64.0)], axis=1)
        .astype(bf16)
        .reshape(nx, ny, 128, 64)
    )
    thirds[0] = dot(dz_third, pick_o).T.astype(bf16)
    thirds[1] = dot(dz_second, pick_o).T.astype(bf16)
    fill(pad_smid, dot(act_second.astype(bf16), pick_mid))
    fill(pad_sin, dot(pooled, pick_in))
    third_i = dot(act_third, pick_mid).astype(bf16)
    lift_o = dot(d_lift, pick_lift).T.astype(bf16)
    g_lift[...] = dot(lift_o, third_i) * scale

    row = lax.broadcasted_iota(jnp.int32, (128, 128), 0)
    lane = lanes_of(128)
    grow = jnp.where(row == lane // 4 + gz * 32, 1.0, 0.0).astype(bf16)
    past = gz * 32 + jnp.where(lane % 2 == 1, -1, 32)
    at_x, at_y = lane // 12, lane // 2 % 6
    rim = jnp.zeros((64, 128), f32)
    for i in range(3):
        for j in range(3):
            x = jnp.clip(gx + i - 1, 0, nx - 1)
            y = jnp.clip(gy + j - 1, 0, ny - 1)
            grown[i, j] = dot_over(table[x, y], grow, (0, 0))
            mine_too = ((at_x + 3) // 4 == i) & ((at_y + 3) // 4 == j) & (lane < 72)
            far = jnp.where((row == past) & mine_too, 1.0, 0.0).astype(bf16)
            rim = rim + dot_over(table[x, y], far, (0, 0))
    swap_finish(*second)

    lane = lanes_of(32)
    at_x, at_y = gx * 4 + lane // 12 - 1, gy * 4 + lane // 2 % 6 - 1
    real = (at_x >= 0) & (at_x < nx * 4) & (at_y >= 0) & (at_y < ny * 4) & (lane < 72)
    reach = gz + jnp.where(lane % 2 == 1, -1, 1)
    real = real & (reach >= 0) & (reach < nz)
    act, bend = silu_parts(columns(got_two, 0))
    near_rim[1] = column_window(jnp.where(real, act + rim[:32], 0.0))
    near_rim[2] = column_window(jnp.where(real, (columns(got_two, 1) + rim[32:]) * bend, 0.0))
    rim_sums[0] = rim_of(ws[2], near_rim[1])
    rim_sums[1] = rim_of(ws[3], near_rim[2])
    dz_edges[...] = jnp.zeros_like(dz_edges)

    def join(r, carry):
        x, y = r // 6, r % 6
        at_x, at_y = gx * 4 + x - 1, gy * 4 + y - 1
        real = (at_x >= 0) & (at_x < nx * 4) & (at_y >= 0) & (at_y < ny * 4)
        keep = jnp.where(real, 1.0, 0.0)
        up = grown[(x + 3) // 4, (y + 3) // 4]
        both = two[x, y].astype(f32)
        act, bend = silu_parts(both[:32])
        joined = (act + up[:32]) * keep
        dz = (both[32:] + up[32:]) * bend * keep
        jd[x, y] = jnp.concatenate([joined, dz]).astype(bf16)
        here = jnp.where((x >= 1) & (x <= 4) & (y >= 1) & (y <= 4), r, -1)
        turned = pltpu.roll(dz, (2 * r + 1) % 128, 1)
        dz_edges[...] = jnp.where(lanes_of(32) // 2 == here, turned, dz_edges[...])
        return carry

    lax.fori_loop(0, 36, join, 0)
    ends = pltpu.roll(pack_one[...].astype(f32), 64, 1)
    ends = jnp.where(lanes_of(32) < 64, ends, 0.0)
    sums[0] = dot_over(near_rim[1], thrice_rim(ends), (1, 1))
    sums[1] = dot_over(near_rim[0], thrice_rim(dz_edges[...]), (1, 1))

    def last(x, carry):
        joined = near(jd, x, slice(0, 32))
        rows = settle(dot(ws[2], joined), rim_sums[0], x)
        for y in range(4):
            tmp[0, pl.ds(y, 32, stride=4), :] = rows[y]
        out[:, x] = tmp[0].reshape(32, 4, 128).astype(bf16)
        given = [one[x + 1, y + 1, 32:64, :] for y in range(4)]
        sums[0] += dot_over(joined, thrice(jnp.concatenate(given, axis=1)), (1, 1))
        rows = settle(dot(ws[3], near(jd, x, slice(32, 64))), rim_sums[1], x)
        for y in range(4):
            tmp[1, pl.ds(y, 32, stride=4), :] = rows[y]
        g_input[:, x] = tmp[1].reshape(32, 4, 128).astype(bf16)
        given = [jd[x + 1, y + 1, 32:64, :] for y in range(4)]
        sums[1] += dot_over(
            near(one, x, slice(0, 32)), thrice(jnp.concatenate(given, axis=1)), (1, 1)
        )
        return carry

    lax.fori_loop(0, 4, last, 0)
    ci, co = 32 // nx, 32 // (ny * nz)
    for f in range(2):
        value = sums[f].reshape(9, nx, ci, 96)
        for i in range(nx):
            turned = value[:, i].reshape(9 * ci, 96).T
            block = jnp.concatenate([turned[:32], turned[32:64], turned[64:]], axis=1)
            for j in range(ny * nz):
                parts[i * ny * nz + j, f * co : f * co + co, :] = block[
                    j * co : j * co + co
                ].astype(bf16)
    each_peer(lambda k: sum_copy(k).start())
    own = pltpu.make_async_copy(parts.at[me], landed.at[me], sum_local)
    own.start()

    taken = []
    for ab in range(9):
        grad = dot(thirds[0], window(pad_smid, ab)) * scale
        share = grad.shape[1] // 3
        for c in range(3):
            g_mid[3 * ab + c] = grad[:, c * share : c * share + share]
        taken.append(dot(thirds[1], window(pad_sin, ab)) * scale)
    chosen = spread(jnp.concatenate(taken, axis=1), chooser_of(ci, 3 * ci, ci))
    for i in range(ci):
        g_in[i] = chosen[:, i * 128 : i * 128 + 27]
    chooser = chooser_of(ci, ci, 9 * ci)
    own.wait()
    each_peer(lambda k: sum_copy(k).wait())
    chosen = spread(landed[...].astype(f32).sum(0) * scale, chooser)
    for i in range(ci):
        g_fine_out[i] = chosen[:co, i * 128 : i * 128 + 27]
        g_fine_in[i] = chosen[co:, i * 128 : i * 128 + 27]


def shards(features, cotangent, w_fine_in, w_coarse_in, w_coarse_mid, w_lift, w_fine_out):
    counts = tuple(lax.axis_size(axis) for axis in AXES)
    nx, ny, nz = counts
    total = nx * ny * nz
    chans, depth, height, length = features.shape
    wide = w_lift.shape[0]
    scale = 1.0 / math.sqrt(total * depth * height * length)
    f32, bf16 = jnp.float32, jnp.bfloat16
    shape = jax.ShapeDtypeStruct
    co, cw = wide // (ny * nz), wide // nx
    ci, fo = chans // nx, chans // (ny * nz)
    pads = [3 * chans, 3 * wide, 3 * cw, 3 * ci]
    block = (2 * fo, 27 * ci)
    rows = pltpu.VMEM((6, 6, 2 * chans, 128), bf16)
    got = pltpu.VMEM((18, chans, 128), bf16)
    packed = pltpu.VMEM((chans, 128), bf16)
    swaps = pltpu.SemaphoreType.DMA((len(SIDES),))
    one, many = pltpu.SemaphoreType.DMA, pltpu.SemaphoreType.DMA((total,))
    anywhere = pl.BlockSpec(memory_space=pl.ANY)
    output, grad_input, g_fine_in, g_in, g_mid, g_lift, g_fine_out = pl.pallas_call(
        lambda *refs: whole_kernel(counts, scale, *refs),
        out_shape=(
            shape(features.shape, bf16),
            shape(features.shape, bf16),
            shape((ci, fo, 27), f32),
            shape((ci, co, 27), f32),
            shape((27, co, cw), f32),
            shape((fo, cw), f32),
            shape((ci, fo, 27), f32),
        ),
        in_specs=vmem(4) + [anywhere] * 2 + vmem(1),
        out_specs=vmem(7),
        scratch_shapes=[
            rows, rows, got, got, packed, packed, swaps, swaps, swaps, swaps,
            pltpu.VMEM((2, 128, 128), f32),
            pltpu.VMEM((4, 3 * chans, 9 * chans), bf16),
            pltpu.VMEM((3, 9 * chans, 128), bf16),
            pltpu.VMEM((2, chans, 128), f32),
            pltpu.VMEM((2 * chans, 128), f32),
            pltpu.VMEM((16, 128), bf16),
            pltpu.VMEM((total, 16, 128), bf16),
            pltpu.VMEM((9, 3 * wide, wide), bf16),
            pltpu.VMEM((9, 3 * wide, chans), bf16),
            pltpu.SemaphoreType.DMA((2,)),
            pltpu.VMEM((9, 3 * chans, wide), bf16),
            pltpu.VMEM((9, 3 * wide, wide), bf16),
            one, many, many,
            pltpu.VMEM((3, 3, 2 * chans, 128), f32),
            pltpu.VMEM((2 * chans, 128), f32),
        ]
        + [pltpu.VMEM((nx + 2, ny + 2, 128, k), bf16) for k in pads]
        + [
            pltpu.VMEM((nx, ny, 128, 2 * chans), bf16),
            pltpu.VMEM((2, co, nx * ny * 128), bf16),
            rows,
            pltpu.VMEM((chans, 128), f32),
            pltpu.VMEM((2, 9 * chans, 3 * chans), f32),
            pltpu.VMEM((total,) + block, bf16),
            pltpu.VMEM((total,) + block, bf16),
            one, many, many,
        ],
        compiler_params=pltpu.CompilerParams(
            collective_id=0, has_side_effects=True, vmem_limit_bytes=ROOMY
        ),
        name="whole",
    )(
        features, cotangent, w_fine_in, w_fine_out,
        w_coarse_in.reshape(9, 3 * chans, wide), w_coarse_mid.reshape(9, 3 * wide, wide), w_lift.T,
    )
    return (
        output,
        grad_input,
        g_fine_in.transpose(2, 0, 1),
        g_in.transpose(2, 0, 1),
        g_mid.transpose(0, 2, 1),
        g_lift.T,
        g_fine_out.transpose(2, 0, 1),
    )


def choose(features, *rest):
    nx, ny, nz = (lax.axis_size(axis) for axis in AXES)
    total = nx * ny * nz
    wide = rest[4].shape[0]
    fits = features.shape == (32, 4, 4, 128) and nz == 4 and total <= DIRECT
    fits = fits and 32 % (ny * nz) == 0 and 32 % nx == 0 and 32 // nx == 8 and wide == 128
    return (shards if fits else shards_layered)(features, *rest)


def solution(mesh):
    whole = P(None, "gx", "gy", "gz")
    split = P(None, "gx", ("gy", "gz"))
    return jax.shard_map(
        choose,
        mesh=mesh,
        in_specs=(whole, whole, P(), P(), P(), P(), P()),
        out_specs=(whole, whole, split, split, split, P("gx", ("gy", "gz")), split),
        check_vma=False,
    )
```

time: 66.8 us -> 50.9 us (0.76)
  Pallas kernels: 56.3 us -> 44.6 us
  local copies, waits for them, and re-layouts: 8.77 us -> 5.42 us
  other arithmetic: 0.73 us -> 0 us
    pallas_call x1, Pallas kernels: 56.3 us -> 44.6 us  [shards(): pl.pallas_call(lambda *refs: whole_kernel(counts, scale, *refs), out_shap...]
    unnamed x21 -> x19, local copies, waits for them, and re-layouts: 7.72 us -> 5.42 us
    transpose x1 -> x0, other arithmetic: 0.73 us -> none  [shards(): rows = jnp.concatenate([features, cotangent]).transpose(1, 2, 0, 3)]
    transpose x1 -> x0, local copies, waits for them, and re-layouts: 0.7 us -> none  [owned(): grad.reshape(9, grad.shape[1], 3, -1).transpose(0, 2, 3, 1)]
where the time goes in v2:
time: 50.9 us; the launch traced here: 50.7 us
  Pallas kernels  44.6 us (88%)
  local copies, waits for them, and re-layouts  5.42 us (11%)
  between operations  0.67 us (1%)
    pallas_call x1, Pallas kernels, shards(): pl.pallas_call(lambda *refs: whole_kernel(counts, scale, *refs), out_shap...  44.6 us
    unnamed x19, local copies, waits for them, and re-layouts  5.42 us

profile of v2, /device:TPU:0, one launch (start us, length us, event | category | flops | bytes accessed | tf_op | source)
XLA Modules:
  0.0 50.7 jit_solution(6611646042503937683)
XLA Ops:
  0.6 44.6 %whole.1 = (bf16[32,4,4,128]{3,2,1,0:T(4,128)(2,1)}, bf16[32,4,4,128]{3,2,1,0:T(4,128)(2,1)}, f32[8,4,27]{2,1,0:T(4,128)}, f32[8,16,27]{2,1,0:T(8,128)}, f32[27,...) custom-call(bf16[32,4,4,128]{3,2,1,0:T(4,128)(2,1)} %refs_0_.1, bf16[32,4,4,128]{3,2,1,0:T(4,128)(2,1)} %refs_1_.1, ...), custom_call_target="tpu_custom_call" | custom-call | tf_op jit(solution)/shard_map/whole/pallas_call | solution.py:723
  45.2 0.0 copy-start.1
  45.2 0.0 copy-start.4
  45.2 1.6 %copy.21 = bf16[32,4,4,128]{3,2,1,0:T(4,128)(2,1)} copy(bf16[32,4,4,128]{3,2,1,0:T(4,128)(2,1)} %get-tuple-element.28) | data formatting | bytes 262144
  46.9 0.0 copy-done.1
  46.9 0.0 copy-start.2
  46.9 0.0 copy-start
  46.9 0.7 %copy.22 = bf16[32,4,4,128]{3,2,1,0:T(4,128)(2,1)} copy(bf16[32,4,4,128]{3,2,1,0:T(4,128)(2,1)S(1)} %copy-done.1) | data formatting | bytes 262144
  47.5 0.0 copy-done.4
  47.6 0.6 %copy.23 = f32[27,8,4]{0,2,1:T(4,128)} copy(f32[27,8,4]{0,2,1:T(4,128)S(1)} %bitcast.13) | data formatting | bytes 6912
  48.2 0.0 copy-done.2
  48.2 0.6 %copy.24 = f32[27,8,16]{0,2,1:T(8,128)} copy(f32[27,8,16]{0,2,1:T(8,128)S(1)} %bitcast.11) | data formatting | bytes 27648
  48.8 0.0 copy-done
  48.8 0.0 copy-start.5
  48.8 0.0 copy-start.3
  48.8 0.7 %copy.25 = f32[27,32,16]{1,2,0:T(8,128)} copy(f32[27,32,16]{1,2,0:T(8,128)S(1)} %bitcast.10) | data formatting | bytes 110592
  49.5 0.0 copy-done.5
  49.5 0.6 %copy.26 = f32[32,4]{0,1:T(4,128)} copy(f32[32,4]{0,1:T(4,128)S(1)} %bitcast.15) | data formatting | bytes 1024
  50.1 0.0 copy-done.3
  50.1 0.6 %copy.27 = f32[27,8,4]{0,2,1:T(4,128)} copy(f32[27,8,4]{0,2,1:T(4,128)S(1)} %bitcast.12) | data formatting | bytes 6912
Async XLA Ops:
  45.2 1.7 %copy-start.1 = (bf16[32,4,4,128]{3,2,1,0:T(4,128)(2,1)S(1)}, bf16[32,4,4,128]{3,2,1,0:T(4,128)(2,1)}, u32[]{:S(2)}) copy-start(bf16[32,4,4,128]{3,2,1,0:T(4,128)(2,1)} %get-tuple-element.29) | copy-start | bytes 393220
  45.2 2.3 %copy-start.4 = (f32[8,4,27]{2,1,0:T(4,128)S(1)}, f32[8,4,27]{2,1,0:T(4,128)}, u32[]{:S(2)}) copy-start(f32[8,4,27]{2,1,0:T(4,128)} %get-tuple-element.16) | copy-start | bytes 10372
  46.9 1.3 %copy-start.2 = (f32[8,16,27]{2,1,0:T(8,128)S(1)}, f32[8,16,27]{2,1,0:T(8,128)}, u32[]{:S(2)}) copy-start(f32[8,16,27]{2,1,0:T(8,128)} %get-tuple-element.17) | copy-start | bytes 41476
  46.9 1.9 %copy-start = (f32[27,16,32]{2,1,0:T(8,128)S(1)}, f32[27,16,32]{2,1,0:T(8,128)}, u32[]{:S(2)}) copy-start(f32[27,16,32]{2,1,0:T(8,128)} %get-tuple-element.18) | copy-start | bytes 165892
  48.8 0.7 %copy-start.5 = (f32[4,32]{1,0:T(4,128)S(1)}, f32[4,32]{1,0:T(4,128)}, u32[]{:S(2)}) copy-start(f32[4,32]{1,0:T(4,128)} %get-tuple-element.19) | copy-start | bytes 1540
  48.8 1.3 %copy-start.3 = (f32[8,4,27]{2,1,0:T(4,128)S(1)}, f32[8,4,27]{2,1,0:T(4,128)}, u32[]{:S(2)}) copy-start(f32[8,4,27]{2,1,0:T(4,128)} %get-tuple-element.20) | copy-start | bytes 10372

commit v3 on v2

--- a/solution.py
+++ b/solution.py
@@ -198,7 +198,8 @@
 
 SIDES = [(i, j, 0) for i in (-1, 0, 1) for j in (-1, 0, 1) if (i, j) != (0, 0)]
 SIDES += [(i, j, k) for i in (-1, 0, 1) for j in (-1, 0, 1) for k in (-1, 1)]
-ROOMY = 60 * 1024 * 1024
+ROOMY = 32 * 1024 * 1024
+HANDED = 4 * 1024 * 1024
 
 
 def vmem(count):
@@ -413,22 +414,25 @@
 
 
 def whole_kernel(
-    counts, scale, fea, cot, w_in, w_out, w_in9, w_mid9, w_lift,
+    counts, scale, fea_far, cot_far, w_in_far, w_out_far, w_in9, w_mid9, w_lift_far,
     out, g_input, g_fine_in, g_in, g_mid, g_lift, g_fine_out,
     one, two, got_one, got_two, pack_one, pack_two, sends_one, recvs_one, sends_two, recvs_two,
     tmp, ws, near_rim, rim_sums, total_ref, mine, full, mid_back, in_back, weight_sems,
     w9, wm9, gather_local, gather_sends, gather_recvs,
     grown, grown_rim, pad_in, pad_mid, pad_smid, pad_sin, table, thirds,
     jd, dz_edges, sums, parts, landed, sum_local, sum_sends, sum_recvs,
+    fea, cot, w_in, w_out, w_lift, ready,
 ):
     nx, ny, nz = counts
     total = nx * ny * nz
     gx, gy, gz = (lax.axis_index(axis) for axis in AXES)
     me = (gx * ny + gy) * nz + gz
     f32, bf16 = jnp.float32, jnp.bfloat16
+    pairs = [(fea_far, fea), (cot_far, cot), (w_in_far, w_in), (w_out_far, w_out)]
+    pairs += [(w_in9, w9), (w_mid9, wm9), (w_lift_far, w_lift)]
     fetches = [
-        pltpu.make_async_copy(w_in9, w9, weight_sems.at[0]),
-        pltpu.make_async_copy(w_mid9, wm9, weight_sems.at[1]),
+        pltpu.make_async_copy(source, target, weight_sems.at[n])
+        for n, (source, target) in enumerate(pairs)
     ]
     for fetch in fetches:
         fetch.start()
@@ -436,14 +440,21 @@
     clear_rim(two, got_two)
     barrier = pltpu.get_barrier_semaphore()
 
-    def greet(k, carry):
-        pl.semaphore_signal(
-            barrier, inc=1, device_id=place((me + k) % total, counts), device_id_type=MESH
-        )
-        return carry
-
-    lax.fori_loop(1, total, greet, 0)
-
+    def tell(semaphore):
+        told = 0
+        for side in SIDES:
+            peer, real = there(counts, side, 1)
+            told = told + jnp.where(real, 1, 0)
+
+            @pl.when(real)
+            def _():
+                pl.semaphore_signal(semaphore, inc=1, device_id=peer, device_id_type=MESH)
+
+        return told
+
+    told = tell(barrier)
+    fetches[0].wait()
+    fetches[1].wait()
     group = jnp.zeros((32, 128), f32)
     for x in range(4):
         tmp[0] = fea[:, x].astype(f32).reshape(128, 128)
@@ -453,11 +464,14 @@
             one[x + 1, y + 1] = jnp.concatenate(values).astype(bf16)
             group = edges(values, x, y, group)
     pack_one[...] = group.astype(bf16)
+    fetches[2].wait()
+    fetches[3].wait()
     ws[0], ws[1], ws[2], ws[3] = ahead(w_in), back(w_out), ahead(w_out), back(w_in)
-    pl.semaphore_wait(barrier, total - 1)
+    pl.semaphore_wait(barrier, told)
     first = (counts, one, pack_one, got_one, sends_one, recvs_one)
     swap_start(*first)
     swap_finish(*first)
+    tell(ready)
 
     for f in range(2):
         window = column_window(columns(got_one, f))
@@ -511,13 +525,14 @@
 
         lax.fori_loop(1, total, step, 0)
 
+    pl.semaphore_wait(ready, told)
     each_peer(lambda k: gather_copy(k).start())
     own = pltpu.make_async_copy(mine, full.at[me], gather_local)
     own.start()
     second = (counts, two, pack_two, got_two, sends_two, recvs_two)
     swap_start(*second)
 
-    for fetch in fetches:
+    for fetch in fetches[4:]:
         fetch.wait()
     wide, narrow = w9.shape[2], in_back.shape[2]
 
@@ -701,6 +716,19 @@
         g_fine_in[i] = chosen[co:, i * 128 : i * 128 + 27]
 
 
+def hand_over(*refs):
+    *refs, sems = refs
+    half = len(refs) // 2
+    copies = [
+        pltpu.make_async_copy(source, target, sems.at[n])
+        for n, (source, target) in enumerate(zip(refs[:half], refs[half:]))
+    ]
+    for copy in copies:
+        copy.start()
+    for copy in copies:
+        copy.wait()
+
+
 def shards(features, cotangent, w_fine_in, w_coarse_in, w_coarse_mid, w_lift, w_fine_out):
     counts = tuple(lax.axis_size(axis) for axis in AXES)
     nx, ny, nz = counts
@@ -720,7 +748,7 @@
     swaps = pltpu.SemaphoreType.DMA((len(SIDES),))
     one, many = pltpu.SemaphoreType.DMA, pltpu.SemaphoreType.DMA((total,))
     anywhere = pl.BlockSpec(memory_space=pl.ANY)
-    output, grad_input, g_fine_in, g_in, g_mid, g_lift, g_fine_out = pl.pallas_call(
+    results = pl.pallas_call(
         lambda *refs: whole_kernel(counts, scale, *refs),
         out_shape=(
             shape(features.shape, bf16),
@@ -731,7 +759,7 @@
             shape((fo, cw), f32),
             shape((ci, fo, 27), f32),
         ),
-        in_specs=vmem(4) + [anywhere] * 2 + vmem(1),
+        in_specs=[pl.BlockSpec(memory_space=pltpu.HBM)] * 7,
         out_specs=vmem(7),
         scratch_shapes=[
             rows, rows, got, got, packed, packed, swaps, swaps, swaps, swaps,
@@ -744,7 +772,7 @@
             pltpu.VMEM((total, 16, 128), bf16),
             pltpu.VMEM((9, 3 * wide, wide), bf16),
             pltpu.VMEM((9, 3 * wide, chans), bf16),
-            pltpu.SemaphoreType.DMA((2,)),
+            pltpu.SemaphoreType.DMA((7,)),
             pltpu.VMEM((9, 3 * chans, wide), bf16),
             pltpu.VMEM((9, 3 * wide, wide), bf16),
             one, many, many,
@@ -761,15 +789,36 @@
             pltpu.VMEM((total,) + block, bf16),
             pltpu.VMEM((total,) + block, bf16),
             one, many, many,
+            pltpu.VMEM(features.shape, bf16),
+            pltpu.VMEM(features.shape, bf16),
+            pltpu.VMEM(w_fine_in.shape, bf16),
+            pltpu.VMEM(w_fine_in.shape, bf16),
+            pltpu.VMEM((chans, wide), bf16),
+            pltpu.SemaphoreType.REGULAR,
         ],
         compiler_params=pltpu.CompilerParams(
             collective_id=0, has_side_effects=True, vmem_limit_bytes=ROOMY
         ),
         name="whole",
     )(
-        features, cotangent, w_fine_in, w_fine_out,
-        w_coarse_in.reshape(9, 3 * chans, wide), w_coarse_mid.reshape(9, 3 * wide, wide), w_lift.T,
-    )
+        *[
+            pltpu.with_memory_space_constraint(value, pltpu.HBM)
+            for value in (
+                features, cotangent, w_fine_in, w_fine_out,
+                w_coarse_in.reshape(9, 3 * chans, wide),
+                w_coarse_mid.reshape(9, 3 * wide, wide), w_lift.T,
+            )
+        ]
+    )
+    output, grad_input, g_fine_in, g_in, g_mid, g_lift, g_fine_out = pl.pallas_call(
+        hand_over,
+        out_shape=[shape(value.shape, value.dtype) for value in results],
+        in_specs=vmem(7),
+        out_specs=[anywhere] * 7,
+        scratch_shapes=[pltpu.SemaphoreType.DMA((7,))],
+        compiler_params=pltpu.CompilerParams(vmem_limit_bytes=HANDED),
+        name="hand_over",
+    )(*results)
     return (
         output,
         grad_input,

time: 50.9 us -> 43.5 us (0.85)
  local copies, waits for them, and re-layouts: 5.42 us -> 0 us
  Pallas kernels: 44.6 us -> 42.7 us
    unnamed x19 -> x0, local copies, waits for them, and re-layouts: 5.42 us -> none
    pallas_call x1, Pallas kernels: 44.6 us -> 41.8 us  [shards(): pl.pallas_call(lambda *refs: whole_kernel(counts, scale, *refs), out_shap...]
    pallas_call x0 -> x1, Pallas kernels: none -> 0.87 us  [shards(): pl.pallas_call(hand_over, out_shape=[shape(value.shape, value.dtype) for...]
where the time goes in v3:
time: 43.5 us; the launch traced here: 43.3 us
  Pallas kernels  42.7 us (98%)
  between operations  0.64 us (1%)
    pallas_call x1, Pallas kernels, shards(): pl.pallas_call(lambda *refs: whole_kernel(counts, scale, *refs), out_shap...  41.8 us

profile of v3, /device:TPU:0, one launch (start us, length us, event | category | flops | bytes accessed | tf_op | source)
XLA Modules:
  0.0 43.3 jit_solution(1175958510477358519)
XLA Ops:
  0.6 41.8 %whole.1 = (bf16[32,4,4,128]{3,2,1,0:T(4,128)(2,1)S(1)}, bf16[32,4,4,128]{3,2,1,0:T(4,128)(2,1)S(1)}, f32[8,4,27]{2,1,0:T(4,128)S(1)}, f32[8,16,27]{2,1,0:T(8,12...) custom-call(bf16[32,4,4,128]{3,2,1,0:T(4,128)(2,1)} %refs_0_.1, ...), custom_call_target="tpu_custom_call" | custom-call | tf_op jit(solution)/shard_map/whole/pallas_call | solution.py:751
  42.4 0.9 %hand_over.1 = (bf16[32,4,4,128]{3,2,1,0:T(4,128)(2,1)}, bf16[32,4,4,128]{3,2,1,0:T(4,128)(2,1)}, f32[8,4,27]{2,1,0:T(4,128)}, f32[8,16,27]{2,1,0:T(8,128)}, f32...) custom-call(bf16[32,4,4,128]{3,2,1,0:T(4,128)(2,1)S(1)} %get-tuple-element.21.refs_0_, ...), custom_call_target="tpu_custom_call" | custom-call | tf_op jit(solution)/shard_map/hand_over/pallas_call | solution.py:813

commit v4 on v3

--- a/solution.py
+++ b/solution.py
@@ -418,10 +418,11 @@
     out, g_input, g_fine_in, g_in, g_mid, g_lift, g_fine_out,
     one, two, got_one, got_two, pack_one, pack_two, sends_one, recvs_one, sends_two, recvs_two,
     tmp, ws, near_rim, rim_sums, total_ref, mine, full, mid_back, in_back, weight_sems,
-    w9, wm9, gather_local, gather_sends, gather_recvs,
+    w9, wm9, gather_local, gather_sems,
     grown, grown_rim, pad_in, pad_mid, pad_smid, pad_sin, table, thirds,
-    jd, dz_edges, sums, parts, landed, sum_local, sum_sends, sum_recvs,
+    jd, dz_edges, sums, parts, landed, sum_local, sum_sems,
     fea, cot, w_in, w_out, w_lift, ready,
+    own_cells, share_a, share_b, land_a, land_b, share_locals, a_sems, b_sems,
 ):
     nx, ny, nz = counts
     total = nx * ny * nz
@@ -501,32 +502,33 @@
     both = jnp.concatenate([means[:, :32] * (1.0 / 64.0), means[:, 32:]], axis=1)
     mine[...] = jnp.concatenate([both[:16], both[16:]], axis=1).astype(bf16)
 
-    def spread_copy(k, source, target, local_sems):
-        peer = (me + k) % total
-        return pltpu.make_async_remote_copy(
-            src_ref=source(peer),
-            dst_ref=target.at[me],
-            send_sem=local_sems[0].at[k],
-            recv_sem=local_sems[1].at[k],
-            device_id=place(peer, counts),
-            device_id_type=MESH,
-        )
-
-    def gather_copy(k):
-        return spread_copy(k, lambda peer: mine, full, (gather_sends, gather_recvs))
-
-    def sum_copy(k):
-        return spread_copy(k, lambda peer: parts.at[peer], landed, (sum_sends, sum_recvs))
-
-    def each_peer(act):
-        def step(k, carry):
-            act(k)
-            return carry
-
-        lax.fori_loop(1, total, step, 0)
+    lines = [
+        [at] + [lax.rem(at + k, count) for k in range(1, count)]
+        for at, count in zip((gx, gy, gz), counts)
+    ]
+
+    def send_all(source, target, sems):
+        for x in reversed(range(nx)):
+            for y in reversed(range(ny)):
+                for z in reversed(range(nz)):
+                    if x + y + z > 0:
+                        peer = (lines[0][x], lines[1][y], lines[2][z])
+                        pltpu.make_async_remote_copy(
+                            src_ref=source(peer[0], peer[1] * nz + peer[2]),
+                            dst_ref=target.at[me],
+                            send_sem=sems.at[0],
+                            recv_sem=sems.at[1],
+                            device_id=peer,
+                            device_id_type=MESH,
+                        ).start()
+
+    def wait_all(target, sems):
+        everyone_else = target.at[pl.ds(0, total - 1)]
+        for n in range(2):
+            pltpu.make_async_copy(everyone_else, everyone_else, sems.at[n]).wait()
 
     pl.semaphore_wait(ready, told)
-    each_peer(lambda k: gather_copy(k).start())
+    send_all(lambda x, o: mine, full, gather_sems)
     own = pltpu.make_async_copy(mine, full.at[me], gather_local)
     own.start()
     second = (counts, two, pack_two, got_two, sends_two, recvs_two)
@@ -547,9 +549,10 @@
     for pad in (pad_in, pad_mid, pad_smid, pad_sin):
         pad[...] = jnp.zeros_like(pad)
     own.wait()
-    each_peer(lambda k: gather_copy(k).wait())
-
-    cells = nx * ny * 128
+    wait_all(full, gather_sems)
+
+    span = 48
+    cells = nx * ny * span
 
     def pick(size, pieces, index):
         each = size // pieces
@@ -558,19 +561,18 @@
         return jnp.where(row == index * each + column, 1.0, 0.0).astype(bf16)
 
     at_o = gy * nz + gz
-    pick_mid, pick_in = pick(128, nx, gx), pick(32, nx, gx)
-    pick_o, pick_lift = pick(128, ny * nz, at_o), pick(32, ny * nz, at_o)
 
     def fill(pad, value):
-        at = lax.broadcasted_iota(jnp.int32, value.shape, 0) % 128
+        rows, size = value.shape[0], pad.shape[2]
+        at = lax.broadcasted_iota(jnp.int32, value.shape, 0) % size
         low = jnp.where(at == 0, 0.0, pltpu.roll(value, 1, 0))
-        high = jnp.where(at == 127, 0.0, pltpu.roll(value, cells - 1, 0))
+        high = jnp.where(at == size - 1, 0.0, pltpu.roll(value, rows - 1, 0))
         wide = jnp.concatenate([low, value, high], axis=1).astype(bf16)
-        pad[1 : nx + 1, 1 : ny + 1] = wide.reshape(nx, ny, 128, wide.shape[1])
+        pad[1 : nx + 1, 1 : ny + 1] = wide.reshape(nx, ny, size, wide.shape[1])
 
     def window(pad, ab):
         a, b = ab // 3, ab % 3
-        return pad[a : a + nx, b : b + ny].reshape(cells, pad.shape[3])
+        return pad[a : a + nx, b : b + ny].reshape(nx * ny * pad.shape[2], pad.shape[3])
 
     def conv(pad, weight):
         result = dot(window(pad, 0), weight[0])
@@ -582,42 +584,53 @@
         sigma = jax.nn.sigmoid(v)
         return sigma * (1.0 + v * (1.0 - sigma))
 
+    before, after = jnp.maximum(gz - 1, 0), jnp.minimum(gz + 1, nz - 1)
     pieces = []
     for k in range(nx * ny):
-        for z in range(nz):
-            block = full[k * nz + z]
-            pieces += [block[:, :64], block[:, 64:]]
-    both = jnp.concatenate(pieces)
-    pooled, d_lift = both[:, :32], both[:, 32:]
-    fill(pad_in, pooled.astype(f32))
+        here = full[k * nz + gz].astype(f32)
+        pieces += [full[k * nz + before].astype(f32)[8:, 64:], here[:, :64], here[:, 64:]]
+        pieces += [full[k * nz + after].astype(f32)[:8, :64]]
+    at_z = lax.broadcasted_iota(jnp.int32, (cells, 128), 0) % span + gz * 32 - 8
+    keep = jnp.where((at_z >= 0) & (at_z < nz * 32), 1.0, 0.0)
+    both = jnp.concatenate(pieces) * keep[:, :64]
+    fill(pad_in, both[:, :32])
     z_second = conv(pad_in, w9)
-    act_second = jax.nn.silu(z_second)
+    act_second = jax.nn.silu(z_second) * keep
     fill(pad_mid, act_second)
     z_third = conv(pad_mid, wm9)
-    act_third = jax.nn.silu(z_third).astype(bf16)
-    lifted = dot(act_third, w_lift[...].T)
-    dz_third = (dot(d_lift, w_lift[...]) * slope(z_third)).astype(bf16)
-    fill(pad_mid, dz_third.astype(f32))
-    dz_second = (conv(pad_mid, mid_back) * slope(z_second)).astype(bf16)
-    fill(pad_mid, dz_second.astype(f32))
+    act_third = jax.nn.silu(z_third)
+    lifted = dot(act_third.astype(bf16), w_lift[...].T)
+    dz_third = dot(both[:, 32:].astype(bf16), w_lift[...]) * slope(z_third) * keep
+    fill(pad_mid, dz_third)
+    dz_second = conv(pad_mid, mid_back) * slope(z_second) * keep
+    fill(pad_mid, dz_second)
     d_pool = conv(pad_mid, in_back)
     table[...] = (
         jnp.concatenate([lifted, d_pool * (1.0 / 64.0)], axis=1)
         .astype(bf16)
-        .reshape(nx, ny, 128, 64)
-    )
-    thirds[0] = dot(dz_third, pick_o).T.astype(bf16)
-    thirds[1] = dot(dz_second, pick_o).T.astype(bf16)
-    fill(pad_smid, dot(act_second.astype(bf16), pick_mid))
-    fill(pad_sin, dot(pooled, pick_in))
-    third_i = dot(act_third, pick_mid).astype(bf16)
-    lift_o = dot(d_lift, pick_lift).T.astype(bf16)
-    g_lift[...] = dot(lift_o, third_i) * scale
-
-    row = lax.broadcasted_iota(jnp.int32, (128, 128), 0)
-    lane = lanes_of(128)
-    grow = jnp.where(row == lane // 4 + gz * 32, 1.0, 0.0).astype(bf16)
-    past = gz * 32 + jnp.where(lane % 2 == 1, -1, 32)
+        .reshape(nx, ny, span, 64)
+    )
+    for n, value in enumerate([act_second, act_third, dz_third, dz_second]):
+        own_cells[:, :, n * 128 : n * 128 + 128] = value.reshape(nx * ny, span, 128)
+    mine_now = own_cells[gx * ny + gy, 8:40, :]
+    wx, wo = 128 // nx, 128 // (ny * nz)
+    for i in range(nx):
+        block = jnp.concatenate(
+            [mine_now[:, n * 128 + i * wx : n * 128 + i * wx + wx] for n in (0, 1)], axis=1
+        )
+        share_a[i] = jnp.concatenate([block[:16], block[16:]], axis=1).astype(bf16)
+    for i in range(ny * nz):
+        block = jnp.concatenate(
+            [mine_now[:, n * 128 + i * wo : n * 128 + i * wo + wo] for n in (2, 3)], axis=1
+        )
+        share_b[i] = jnp.concatenate(
+            [block[8 * q : 8 * q + 8] for q in range(4)], axis=1
+        ).astype(bf16)
+
+    row = lax.broadcasted_iota(jnp.int32, (span, 128), 0)
+    lane = lanes_of(span)
+    grow = jnp.where(row == lane // 4 + 8, 1.0, 0.0).astype(bf16)
+    past = 8 + jnp.where(lane % 2 == 1, -1, 32)
     at_x, at_y = lane // 12, lane // 2 % 6
     rim = jnp.zeros((64, 128), f32)
     for i in range(3):
@@ -628,6 +641,14 @@
             mine_too = ((at_x + 3) // 4 == i) & ((at_y + 3) // 4 == j) & (lane < 72)
             far = jnp.where((row == past) & mine_too, 1.0, 0.0).astype(bf16)
             rim = rim + dot_over(table[x, y], far, (0, 0))
+    send_all(lambda x, o: share_a.at[x], land_a, a_sems)
+    send_all(lambda x, o: share_b.at[o], land_b, b_sems)
+    owns = [
+        pltpu.make_async_copy(share_a.at[gx], land_a.at[me], share_locals.at[0]),
+        pltpu.make_async_copy(share_b.at[at_o], land_b.at[me], share_locals.at[1]),
+    ]
+    for copy in owns:
+        copy.start()
     swap_finish(*second)
 
     lane = lanes_of(32)
@@ -693,10 +714,31 @@
                 parts[i * ny * nz + j, f * co : f * co + co, :] = block[
                     j * co : j * co + co
                 ].astype(bf16)
-    each_peer(lambda k: sum_copy(k).start())
+    send_all(lambda x, o: parts.at[x * (ny * nz) + o], landed, sum_sems)
     own = pltpu.make_async_copy(parts.at[me], landed.at[me], sum_local)
     own.start()
 
+    for copy in owns:
+        copy.wait()
+    wait_all(land_a, a_sems)
+    wait_all(land_b, b_sems)
+    pieces, firsts, seconds = [], [], []
+    for k in range(total):
+        block = full[k]
+        pieces += [block[:, :64], block[:, 64:]]
+        block = land_a[k].astype(f32)
+        firsts += [block[:, :64], block[:, 64:]]
+        block = land_b[k].astype(f32)
+        seconds += [block[:, 32 * q : 32 * q + 32] for q in range(4)]
+    both = jnp.concatenate(pieces)
+    pooled, d_lift = both[:, :32], both[:, 32:]
+    acts = jnp.concatenate(firsts)
+    fill(pad_smid, acts[:, :32])
+    fill(pad_sin, dot(pooled, pick(32, nx, gx)))
+    turned = jnp.concatenate(seconds).T.astype(bf16)
+    thirds[0], thirds[1] = turned[:16], turned[16:]
+    lift_o = dot(d_lift, pick(32, ny * nz, at_o)).T.astype(bf16)
+    g_lift[...] = dot(lift_o, acts[:, 32:].astype(bf16)) * scale
     taken = []
     for ab in range(9):
         grad = dot(thirds[0], window(pad_smid, ab)) * scale
@@ -709,7 +751,7 @@
         g_in[i] = chosen[:, i * 128 : i * 128 + 27]
     chooser = chooser_of(ci, ci, 9 * ci)
     own.wait()
-    each_peer(lambda k: sum_copy(k).wait())
+    wait_all(landed, sum_sems)
     chosen = spread(landed[...].astype(f32).sum(0) * scale, chooser)
     for i in range(ci):
         g_fine_out[i] = chosen[:co, i * 128 : i * 128 + 27]
@@ -746,7 +788,7 @@
     got = pltpu.VMEM((18, chans, 128), bf16)
     packed = pltpu.VMEM((chans, 128), bf16)
     swaps = pltpu.SemaphoreType.DMA((len(SIDES),))
-    one, many = pltpu.SemaphoreType.DMA, pltpu.SemaphoreType.DMA((total,))
+    one, both_ways = pltpu.SemaphoreType.DMA, pltpu.SemaphoreType.DMA((2,))
     anywhere = pl.BlockSpec(memory_space=pl.ANY)
     results = pl.pallas_call(
         lambda *refs: whole_kernel(counts, scale, *refs),
@@ -775,26 +817,36 @@
             pltpu.SemaphoreType.DMA((7,)),
             pltpu.VMEM((9, 3 * chans, wide), bf16),
             pltpu.VMEM((9, 3 * wide, wide), bf16),
-            one, many, many,
+            one, both_ways,
             pltpu.VMEM((3, 3, 2 * chans, 128), f32),
             pltpu.VMEM((2 * chans, 128), f32),
         ]
-        + [pltpu.VMEM((nx + 2, ny + 2, 128, k), bf16) for k in pads]
         + [
-            pltpu.VMEM((nx, ny, 128, 2 * chans), bf16),
+            pltpu.VMEM((nx + 2, ny + 2, z, k), bf16)
+            for z, k in zip((48, 48, 128, 128), pads)
+        ]
+        + [
+            pltpu.VMEM((nx, ny, 48, 2 * chans), bf16),
             pltpu.VMEM((2, co, nx * ny * 128), bf16),
             rows,
             pltpu.VMEM((chans, 128), f32),
             pltpu.VMEM((2, 9 * chans, 3 * chans), f32),
             pltpu.VMEM((total,) + block, bf16),
             pltpu.VMEM((total,) + block, bf16),
-            one, many, many,
+            one, both_ways,
             pltpu.VMEM(features.shape, bf16),
             pltpu.VMEM(features.shape, bf16),
             pltpu.VMEM(w_fine_in.shape, bf16),
             pltpu.VMEM(w_fine_in.shape, bf16),
             pltpu.VMEM((chans, wide), bf16),
             pltpu.SemaphoreType.REGULAR,
+            pltpu.VMEM((nx * ny, 48, 4 * wide), f32),
+            pltpu.VMEM((nx, 16, 128), bf16),
+            pltpu.VMEM((ny * nz, 8, 128), bf16),
+            pltpu.VMEM((total, 16, 128), bf16),
+            pltpu.VMEM((total, 8, 128), bf16),
+            pltpu.SemaphoreType.DMA((2,)),
+            both_ways, both_ways,
         ],
         compiler_params=pltpu.CompilerParams(
             collective_id=0, has_side_effects=True, vmem_limit_bytes=ROOMY
@@ -835,7 +887,7 @@
     total = nx * ny * nz
     wide = rest[4].shape[0]
     fits = features.shape == (32, 4, 4, 128) and nz == 4 and total <= DIRECT
-    fits = fits and 32 % (ny * nz) == 0 and 32 % nx == 0 and 32 // nx == 8 and wide == 128
+    fits = fits and 32 % (ny * nz) == 0 and 32 % nx == 0 and 32 // nx == 8 and ny * nz == 8 and wide == 128
     return (shards if fits else shards_layered)(features, *rest)
 
 

time: 43.5 us -> 37.3 us (0.86)
  Pallas kernels: 42.7 us -> 36.5 us
    pallas_call x1, Pallas kernels: 41.8 us -> 35.6 us  [shards(): pl.pallas_call(lambda *refs: whole_kernel(counts, scale, *refs), out_shap...]
where the time goes in v4:
time: 37.3 us; the launch traced here: 37.1 us
  Pallas kernels  36.5 us (98%)
  between operations  0.64 us (2%)
    pallas_call x1, Pallas kernels, shards(): pl.pallas_call(lambda *refs: whole_kernel(counts, scale, *refs), out_shap...  35.6 us
    pallas_call x1, Pallas kernels, shards(): pl.pallas_call(hand_over, out_shape=[shape(value.shape, value.dtype) for...  0.87 us

profile of v4, /device:TPU:0, one launch (start us, length us, event | category | flops | bytes accessed | tf_op | source)
XLA Modules:
  0.0 37.1 jit_solution(11563791767732589395)
XLA Ops:
  0.6 35.6 %whole.1 = (bf16[32,4,4,128]{3,2,1,0:T(4,128)(2,1)S(1)}, bf16[32,4,4,128]{3,2,1,0:T(4,128)(2,1)S(1)}, f32[8,4,27]{2,1,0:T(4,128)S(1)}, f32[8,16,27]{2,1,0:T(8,12...) custom-call(bf16[32,4,4,128]{3,2,1,0:T(4,128)(2,1)} %refs_0_.1, ...), custom_call_target="tpu_custom_call" | custom-call | tf_op jit(solution)/shard_map/whole/pallas_call | solution.py:793
  36.2 0.9 %hand_over.1 = (bf16[32,4,4,128]{3,2,1,0:T(4,128)(2,1)}, bf16[32,4,4,128]{3,2,1,0:T(4,128)(2,1)}, f32[8,4,27]{2,1,0:T(4,128)}, f32[8,16,27]{2,1,0:T(8,128)}, f32...) custom-call(bf16[32,4,4,128]{3,2,1,0:T(4,128)(2,1)S(1)} %get-tuple-element.21.refs_0_, ...), custom_call_target="tpu_custom_call" | custom-call | tf_op jit(solution)/shard_map/hand_over/pallas_call | solution.py:865

commit v5 on v4

--- a/solution.py
+++ b/solution.py
@@ -438,7 +438,6 @@
     for fetch in fetches:
         fetch.start()
     clear_rim(one, got_one)
-    clear_rim(two, got_two)
     barrier = pltpu.get_barrier_semaphore()
 
     def tell(semaphore):
@@ -454,6 +453,7 @@
         return told
 
     told = tell(barrier)
+    clear_rim(two, got_two)
     fetches[0].wait()
     fetches[1].wait()
     group = jnp.zeros((32, 128), f32)
@@ -663,23 +663,26 @@
     rim_sums[1] = rim_of(ws[3], near_rim[2])
     dz_edges[...] = jnp.zeros_like(dz_edges)
 
-    def join(r, carry):
-        x, y = r // 6, r % 6
-        at_x, at_y = gx * 4 + x - 1, gy * 4 + y - 1
-        real = (at_x >= 0) & (at_x < nx * 4) & (at_y >= 0) & (at_y < ny * 4)
-        keep = jnp.where(real, 1.0, 0.0)
-        up = grown[(x + 3) // 4, (y + 3) // 4]
-        both = two[x, y].astype(f32)
-        act, bend = silu_parts(both[:32])
-        joined = (act + up[:32]) * keep
-        dz = (both[32:] + up[32:]) * bend * keep
-        jd[x, y] = jnp.concatenate([joined, dz]).astype(bf16)
-        here = jnp.where((x >= 1) & (x <= 4) & (y >= 1) & (y <= 4), r, -1)
-        turned = pltpu.roll(dz, (2 * r + 1) % 128, 1)
-        dz_edges[...] = jnp.where(lanes_of(32) // 2 == here, turned, dz_edges[...])
+    def join(x, carry):
+        group = dz_edges[...]
+        for y in range(6):
+            at_x, at_y = gx * 4 + x - 1, gy * 4 + y - 1
+            real = (at_x >= 0) & (at_x < nx * 4) & (at_y >= 0) & (at_y < ny * 4)
+            keep = jnp.where(real, 1.0, 0.0)
+            up = grown[(x + 3) // 4, (y + 3) // 4]
+            both = two[x, y].astype(f32)
+            act, bend = silu_parts(both[:32])
+            joined = (act + up[:32]) * keep
+            dz = (both[32:] + up[32:]) * bend * keep
+            jd[x, y] = jnp.concatenate([joined, dz]).astype(bf16)
+            if 1 <= y <= 4:
+                here = jnp.where((x >= 1) & (x <= 4), x * 6 + y, -1)
+                turned = pltpu.roll(dz, (12 * x + 2 * y + 1) % 128, 1)
+                group = jnp.where(lanes_of(32) // 2 == here, turned, group)
+        dz_edges[...] = group
         return carry
 
-    lax.fori_loop(0, 36, join, 0)
+    lax.fori_loop(0, 6, join, 0)
     ends = pltpu.roll(pack_one[...].astype(f32), 64, 1)
     ends = jnp.where(lanes_of(32) < 64, ends, 0.0)
     sums[0] = dot_over(near_rim[1], thrice_rim(ends), (1, 1))

time: 37.3 us -> 36.2 us (0.971)
  Pallas kernels: 36.5 us -> 35.5 us
    pallas_call x1, Pallas kernels: 35.6 us -> 34.6 us  [shards(): pl.pallas_call(lambda *refs: whole_kernel(counts, scale, *refs), out_shap...]
where the time goes in v5:
time: 36.2 us; the launch traced here: 36.1 us
  Pallas kernels  35.5 us (98%)
  between operations  0.64 us (2%)
    pallas_call x1, Pallas kernels, shards(): pl.pallas_call(lambda *refs: whole_kernel(counts, scale, *refs), out_shap...  34.6 us
    pallas_call x1, Pallas kernels, shards(): pl.pallas_call(hand_over, out_shape=[shape(value.shape, value.dtype) for...  0.87 us

profile of v5, /device:TPU:0, one launch (start us, length us, event | category | flops | bytes accessed | tf_op | source)
XLA Modules:
  0.0 36.1 jit_solution(13205420116059420916)
XLA Ops:
  0.6 34.6 %whole.1 = (bf16[32,4,4,128]{3,2,1,0:T(4,128)(2,1)S(1)}, bf16[32,4,4,128]{3,2,1,0:T(4,128)(2,1)S(1)}, f32[8,4,27]{2,1,0:T(4,128)S(1)}, f32[8,16,27]{2,1,0:T(8,12...) custom-call(bf16[32,4,4,128]{3,2,1,0:T(4,128)(2,1)} %refs_0_.1, ...), custom_call_target="tpu_custom_call" | custom-call | tf_op jit(solution)/shard_map/whole/pallas_call | solution.py:796
  35.2 0.9 %hand_over.1 = (bf16[32,4,4,128]{3,2,1,0:T(4,128)(2,1)}, bf16[32,4,4,128]{3,2,1,0:T(4,128)(2,1)}, f32[8,4,27]{2,1,0:T(4,128)}, f32[8,16,27]{2,1,0:T(8,128)}, f32...) custom-call(bf16[32,4,4,128]{3,2,1,0:T(4,128)(2,1)S(1)} %get-tuple-element.21.refs_0_, ...), custom_call_target="tpu_custom_call" | custom-call | tf_op jit(solution)/shard_map/hand_over/pallas_call | solution.py:868

commit v6 on v5

--- a/solution.py
+++ b/solution.py
@@ -495,7 +495,8 @@
         total_ref[...] += jnp.concatenate([acts, d[0] + d[1] + d[2] + d[3]])
         return carry
 
-    lax.fori_loop(0, 4, fine, 0)
+    for x in range(4):
+        fine(x, 0)
     row = lax.broadcasted_iota(jnp.int32, (32, 128), 0)
     pick_cell = jnp.where(lanes_of(32) // 4 == row, 1.0, 0.0)
     means = dot_over(pick_cell, total_ref[...], (1, 1), lax.Precision.HIGHEST)
@@ -682,7 +683,8 @@
         dz_edges[...] = group
         return carry
 
-    lax.fori_loop(0, 6, join, 0)
+    for x in range(6):
+        join(x, 0)
     ends = pltpu.roll(pack_one[...].astype(f32), 64, 1)
     ends = jnp.where(lanes_of(32) < 64, ends, 0.0)
     sums[0] = dot_over(near_rim[1], thrice_rim(ends), (1, 1))

time: 36.2 us -> 35.8 us (0.989)
  Pallas kernels: 35.5 us -> 35 us
    pallas_call x1, Pallas kernels: 34.6 us -> 34.2 us  [shards(): pl.pallas_call(lambda *refs: whole_kernel(counts, scale, *refs), out_shap...]
where the time goes in v6:
time: 35.8 us; the launch traced here: 35.7 us
  Pallas kernels  35 us (98%)
  between operations  0.64 us (2%)
    pallas_call x1, Pallas kernels, shards(): pl.pallas_call(lambda *refs: whole_kernel(counts, scale, *refs), out_shap...  34.2 us
    pallas_call x1, Pallas kernels, shards(): pl.pallas_call(hand_over, out_shape=[shape(value.shape, value.dtype) for...  0.87 us

profile of v6, /device:TPU:0, one launch (start us, length us, event | category | flops | bytes accessed | tf_op | source)
XLA Modules:
  0.0 35.7 jit_solution(10461095147747313974)
XLA Ops:
  0.6 34.2 %whole.1 = (bf16[32,4,4,128]{3,2,1,0:T(4,128)(2,1)S(1)}, bf16[32,4,4,128]{3,2,1,0:T(4,128)(2,1)S(1)}, f32[8,4,27]{2,1,0:T(4,128)S(1)}, f32[8,16,27]{2,1,0:T(8,12...) custom-call(bf16[32,4,4,128]{3,2,1,0:T(4,128)(2,1)} %refs_0_.1, ...), custom_call_target="tpu_custom_call" | custom-call | tf_op jit(solution)/shard_map/whole/pallas_call | solution.py:798
  34.8 0.9 %hand_over.1 = (bf16[32,4,4,128]{3,2,1,0:T(4,128)(2,1)}, bf16[32,4,4,128]{3,2,1,0:T(4,128)(2,1)}, f32[8,4,27]{2,1,0:T(4,128)}, f32[8,16,27]{2,1,0:T(8,128)}, f32...) custom-call(bf16[32,4,4,128]{3,2,1,0:T(4,128)(2,1)S(1)} %get-tuple-element.21.refs_0_, ...), custom_call_target="tpu_custom_call" | custom-call | tf_op jit(solution)/shard_map/hand_over/pallas_call | solution.py:870
